TPU v7x, 32 devices: a whole 2x2x4 slice. The times are simulated.
32 devices in a mesh: leaf: 8 (over z, y), sub: 4 (over x, core).
Axes of the slice: x: 2, y: 2, z: 4, core: 2. Of those that a mesh axis runs over, the one named last changes fastest.
Arguments:
- points: float32 [2048, 8, 128], P(('leaf', 'sub')), may hold values from -6 to 6
- probes: bfloat16 [2048, 32, 128], P(('leaf', 'sub')), may hold values from -6 to 6
- leaf_basis: bfloat16 [2048, 64, 128], P(('leaf', 'sub')), may hold values from -0.5 to 0.5
- mid_transfer: float32 [2048, 64, 64], P(('leaf', 'sub')), may hold values from -0.25 to 0.25
- top_transfer: float32 [256, 64, 64], P(('leaf', 'sub')), may hold values from -0.25 to 0.25
- mid_skeleton: float32 [256, 8, 64], P(('leaf', 'sub')), may hold values from -6 to 6
- top_skeleton: float32 [8, 8, 64], replicated, may hold values from -6 to 6
- near_list: int32 [2048, 8], P(('leaf', 'sub')), may hold values from -1 to 2047, as said below
- mid_list: int32 [256, 6], P(('leaf', 'sub')), may hold values from -1 to 255, as said below
- top_list: int32 [8, 6], P('leaf'), may hold values from -1 to 7, as said below
- inv_scale: float32 [8], replicated, may hold values from 0.15 to 0.5
- amplitude: float32 [1], replicated, may hold values from 0.03 to 0.1
- noise_var: float32 [1], replicated, may hold values from 0.2 to 1
Outputs:
- first_product: bfloat16 [2048, 32, 128], P(('leaf', 'sub'))
- second_product: bfloat16 [2048, 32, 128], P(('leaf', 'sub'))
Inputs may be any that keep to these rules, and one draw needn't show every extreme that they name: `near_list`: entry 0 of row i is i; the other entries of a row are distinct leaves j != i with |j - i| <= 64, or -1. `mid_list`: the entries of a row m are distinct middle clusters j != m with |j - m| <= 8, or -1. `top_list`: the entries of a row t are distinct top clusters other than t, or -1.
All inputs are finite; a program needn't handle non-finite values.
Results may differ from a plain program's by a relative error of at most 0.0042.
Values may be sent and summed in bfloat16 or wider, within the bound.
No kernel may reach another device: no remote copies, remote signals or barrier semaphores. Data moves between devices by JAX's collectives and lax.ppermute only.
A program may use at most 128 MiB of HBM per device.

v0:
```python
import jax
import jax.numpy as jnp
from jax import lax
from jax.sharding import PartitionSpec as P

MATVECS = 2


def padded(block, sides, width):
    for axis, dim in sides:
        count = lax.axis_size(axis)
        forward = [(i, i + 1) for i in range(count - 1)]
        backward = [(target, source) for source, target in forward]
        low = lax.ppermute(
            lax.slice_in_dim(block, block.shape[dim] - width, None, axis=dim), axis, forward
        )
        high = lax.ppermute(lax.slice_in_dim(block, 0, width, axis=dim), axis, backward)
        block = jnp.concatenate([low, block, high], axis=dim)
    return block


def matern(left_side, right_side, inv_scale, amplitude):
    accumulated = None
    for feature in range(left_side.shape[-2]):
        difference = (
            left_side[..., feature, :, None] - right_side[..., feature, None, :]
        ) * inv_scale[feature]
        if accumulated is None:
            accumulated = difference * difference
        else:
            accumulated = accumulated + difference * difference
    scaled = jnp.sqrt(3.0 * accumulated)
    return amplitude * (1.0 + scaled) * jnp.exp(-scaled)


def on_device(
    points,
    probes,
    leaf_basis,
    mid_transfer,
    top_transfer,
    mid_skeleton,
    top_skeleton,
    near_list,
    mid_list,
    top_list,
    inv_scale,
    amplitude,
    noise_var,
):
    highest = lax.Precision.HIGHEST
    scale_amp = amplitude[0]
    leaf_dev = points.shape[0]
    mid_dev = mid_skeleton.shape[0]
    probe_count = probes.shape[1]
    rank = leaf_basis.shape[1]
    position = lax.axis_index("leaf") * lax.axis_size("sub") + lax.axis_index("sub")
    leaf_start = position * leaf_dev
    mid_start = position * mid_dev
    top_index = lax.axis_index("leaf")
    wide_points = padded(points, ((("leaf", "sub"), 0),), leaf_dev)
    near_present = near_list >= 0
    near_local = jnp.where(near_present, near_list - leaf_start + leaf_dev, 0)
    near_blocks = matern(points[:, None], wide_points[near_local], inv_scale, scale_amp)
    near_blocks = (near_blocks * near_present[:, :, None, None].astype(jnp.float32)).astype(
        jnp.bfloat16
    )
    wide_skeleton = padded(mid_skeleton, ((("leaf", "sub"), 0),), mid_dev)
    mid_present = mid_list >= 0
    mid_local_ids = jnp.where(mid_present, mid_list - mid_start + mid_dev, 0)
    mid_coupling = matern(mid_skeleton[:, None], wide_skeleton[mid_local_ids], inv_scale, scale_amp)
    mid_coupling = mid_coupling * mid_present[:, :, None, None].astype(jnp.float32)
    top_row = top_list[0]
    top_present = top_row >= 0
    top_clipped = jnp.where(top_present, top_row, 0)
    own_skeleton = lax.dynamic_index_in_dim(top_skeleton, top_index, 0, keepdims=True)
    top_coupling = matern(own_skeleton, top_skeleton[top_clipped], inv_scale, scale_amp)
    top_coupling = top_coupling * top_present[:, None, None].astype(jnp.float32)
    transfer_groups = mid_transfer.reshape(mid_dev, -1, rank, rank)
    vector = probes
    results = []
    for matvec_turn in range(MATVECS):
        leaf_coef = jnp.einsum(
            "lpn,lrn->lpr", vector, leaf_basis, preferred_element_type=jnp.float32
        )
        leaf_groups = leaf_coef.reshape(mid_dev, -1, probe_count, rank)
        mid_coef = jnp.einsum("mcpr,mcrs->mps", leaf_groups, transfer_groups, precision=highest)
        wide_coef = padded(mid_coef, ((("leaf", "sub"), 0),), mid_dev)
        mid_local = jnp.einsum(
            "mkrs,mkps->mpr", mid_coupling, wide_coef[mid_local_ids], precision=highest
        )
        partial_top = jnp.einsum("mpr,mrs->ps", mid_coef, top_transfer, precision=highest)
        group_total = lax.psum(partial_top, "sub")
        all_top = lax.all_gather(group_total[None], "leaf", axis=0, tiled=True)
        top_local = jnp.einsum("krs,kps->pr", top_coupling, all_top[top_clipped], precision=highest)
        mid_total = mid_local + jnp.einsum(
            "ps,mrs->mpr", top_local, top_transfer, precision=highest
        )
        leaf_total = jnp.einsum("mps,mcrs->mcpr", mid_total, transfer_groups, precision=highest)
        leaf_total = leaf_total.reshape(leaf_dev, probe_count, rank).astype(jnp.bfloat16)
        far = jnp.einsum("lpr,lrn->lpn", leaf_total, leaf_basis, preferred_element_type=jnp.float32)
        wide_vector = padded(vector, ((("leaf", "sub"), 0),), leaf_dev)
        near = jnp.einsum(
            "iknm,ikpm->ipn",
            near_blocks,
            wide_vector[near_local],
            preferred_element_type=jnp.float32,
        )
        vector = (noise_var[0] * vector.astype(jnp.float32) + near + far).astype(jnp.bfloat16)
        results.append(vector)
    return (results[0], results[1])


def solution(mesh):
    in_specs = (
        P(("leaf", "sub"), None, None),
        P(("leaf", "sub"), None, None),
        P(("leaf", "sub"), None, None),
        P(("leaf", "sub"), None, None),
        P(("leaf", "sub"), None, None),
        P(("leaf", "sub"), None, None),
        P(),
        P(("leaf", "sub"), None),
        P(("leaf", "sub"), None),
        P("leaf", None),
        P(),
        P(),
        P(),
    )
    out_specs = (P(("leaf", "sub"), None, None), P(("leaf", "sub"), None, None))
    return jax.shard_map(
        on_device, mesh=mesh, in_specs=in_specs, out_specs=out_specs, check_vma=False
    )
```

profile of v0, /device:TPU:0, one launch (start us, length us, event | category | flops | bytes accessed | tf_op | source)
XLA Modules:
  0.0 394.4 jit_solution(14680533488961972634)
XLA Ops:
  2.1 3.9 collective-permute-start
  7.2 4.3 %collective-permute-start.6 = (f32[8,8,64]{2,1,0:T(8,128)}, f32[8,8,64]{2,1,0:T(8,128)S(1)}, u32[]{:S(2)}, u32[]{:S(2)}) collective-permute-start(f32[8,8,64]{2,1,0:T(8,128)} %param.18), channel_id=1, source_target_pairs={{0,1},{1,2},{2,3},{3,4},{4,5},{5,6},{6,7},{7,8},{8,9},{9,10},{10,1... | collective-permute-start | bytes 49160 | tf_op jit(solution)/shard_map/ppermute | solution.py:14
  17.4 3.3 fusion.23
  25.2 15.2 %psum.14 = f32[1,32,64]{2,1,0:T(8,128)S(1)} all-reduce(f32[1,32,64]{2,1,0:T(8,128)S(1)} %convolution_bitcast_fusion.9), channel_id=1, replica_groups=mesh['leaf'=8,'sub'=4] {'sub'}, use_global_device_ids=true, to_apply=%region_0.1 | all-reduce | flops 2048 | bytes 16384 | tf_op jit(solution)/shard_map/psum | solution.py:93
  40.4 33.7 %all_gather.6 = f32[8,32,64]{2,1,0:T(8,128)S(1)} all-gather(f32[1,32,64]{2,1,0:T(8,128)S(1)} %psum.14), channel_id=1, replica_groups=mesh['leaf'=8,'sub'=4] {'leaf'}, dimensions={0}, use_global_device_ids=true | all-gather | bytes 73728 | tf_op jit(solution)/shard_map/all_gather | solution.py:94
  76.0 5.7 %fusion.9 = f32[32,64,1]{1,0,2:T(8,128)S(1)} fusion(f32[6,32,64]{2,1,0:T(8,128)S(1)} %gather_fusion.4, f32[6]{0:T(128)S(1)} %fusion.12, f32[]{:T(128)} %bitcast.28, f32[6,64]{1,0:T(8,128)S(1)} %get-tuple-element.58, f32[64]{0:T(128)S(1)} %get-tuple-element.43, f32[]{:T(128)} %bitcast.25, f32[6,64]{1,0:T(8,128)S(1)} %get-tuple-element.59, ...), kind=kOutput, calls=%fused_computation.41 | convolution fusion | flops 10346496 | bytes 71740 | tf_op jit(solution)/shard_map/krs,kps->pr/dot_general | solution.py:95
  86.5 3.7 collective-permute-start.4
  98.3 10.5 %fusion.5 = f32[8,32,64,1]{2,1,3,0:T(8,128)S(1)} fusion(f32[8,32,64]{2,1,0:T(8,128)S(1)} %convolution_bitcast_fusion.6, f32[8,6,32,64]{3,2,1,0:T(8,128)} %bitcast.218, f32[8,6]{1,0:T(8,128)} %fusion.10, f32[]{:T(128)} %bitcast.28, f32[8,6,64]{2,1,0:T(8,128)} %get-tuple-element.66, f32[8,64]{1,0:T(8,128)} %bitcast.255, f32[]{:T(128)} %bitcast.25, ...), kind=kOutput, calls=%fused_computation.26 | convolution fusion | flops 82788352 | bytes 639204 | tf_op jit(solution)/shard_map/mkrs,mkps->mpr/dot_general | solution.py:89
  108.7 6.6 %convolution_convert_fusion.1 = bf16[8,32,8,64]{3,1,2,0:T(8,128)(2,1)} fusion(f32[8,32,64,1]{2,1,3,0:T(8,128)S(1)} %fusion.5, f32[8,8,64,64]{3,2,1,0:T(8,128)S(1)} %bitcast.206), kind=kOutput, calls=%fused_computation.22 | convolution fusion | flops 100794368 | bytes 1376256 | tf_op jit(solution)/shard_map/mps,mcrs->mcpr/dot_general | solution.py:99
  119.8 8.9 %fusion.22 = (f32[64,8,1,128]{3,2,1,0:T(1,128)S(1)}, f32[64,8,1,128]{3,2,1,0:T(1,128)S(1)}, f32[64,8,1,128]{3,2,1,0:T(1,128)S(1)}, f32[64,8,1,128]{3,2,1,0:T(1,1...) fusion(f32[64,8,8,128]{3,2,1,0:T(8,128)} %bitcast.211), kind=kLoop, calls=%fused_computation.89 | loop fusion | bytes 4194304 | tf_op jit(solution)/shard_map/slice | solution.py:26
  128.8 63.6 %multiply_convert_fusion.6 = bf16[64,8,128,128]{3,2,1,0:T(8,128)(2,1)} fusion(f32[64,8]{1,0:T(8,128)S(1)} %copy-done.16, f32[]{:T(128)} %bitcast.28, f32[64,8,128]{2,1,0:T(8,128)S(1)} %bitcast.234, f32[64,128]{1,0:T(8,128)S(1)} %bitcast.239, f32[]{:T(128)} %bitcast.25, f32[64,8,128]{2,1,0:T(8,128)S(1)} %bitcast.222, f32[64,128]{1,0:T(8,128)S(1)} %bitcast.241, ...), kind=kLoop, calls=%fused_computation.9.clone.1.clone | loop fusion | flops 318767104 | bytes 19138596 | tf_op jit(solution)/shard_map/iknm,ikpm->ipn/dot_general | solution.py:103
  192.4 63.8 %multiply_convert_fusion.5 = bf16[64,8,128,128]{3,2,1,0:T(8,128)(2,1)} fusion(f32[64,8]{1,0:T(8,128)S(1)} %copy-done.16, f32[]{:T(128)} %bitcast.28, f32[64,8,128]{2,1,0:T(8,128)S(1)} %bitcast.235, f32[64,128]{1,0:T(8,128)S(1)} %bitcast.240, f32[]{:T(128)} %bitcast.25, f32[64,8,128]{2,1,0:T(8,128)S(1)} %bitcast.223, f32[64,128]{1,0:T(8,128)S(1)} %bitcast.242, ...), kind=kLoop, calls=%fused_computation.9.clone.clone.1 | loop fusion | flops 318767104 | bytes 19138596 | tf_op jit(solution)/shard_map/iknm,ikpm->ipn/dot_general | solution.py:103
  258.8 4.7 %gather_fusion = bf16[512,32,128]{2,1,0:T(8,128)(2,1)} fusion(bf16[192,32,128]{2,1,0:T(8,128)(2,1)} %pad_maximum_fusion, s32[1024]{0:T(1024)S(1)} %pad_clamp_fusion.2), kind=kCustom, calls=%fused_computation | custom fusion | bytes 8390656 | tf_op jit(solution)/shard_map/gather | solution.py:106
  263.5 13.9 %fusion.1 = f32[64,32,128]{2,1,0:T(8,128)} fusion(bf16[64,8,32,128]{3,2,1,0:T(8,128)(2,1)} %bitcast.210, bf16[64,32,128]{2,1,0:T(8,128)(2,1)} %param.14, f32[]{:T(128)} %bitcast.203, bf16[64,8,128,128]{3,2,1,0:T(8,128)(2,1)} %multiply_convert_fusion.6), kind=kOutput, calls=%fused_computation.18 | convolution fusion | flops 537657344 | bytes 22544388 | tf_op jit(solution)/shard_map/iknm,ikpm->ipn/dot_general | solution.py:103
  281.2 3.8 collective-permute-start.8
  290.3 3.7 collective-permute-start.10
  294.0 13.4 %psum.15 = f32[1,32,64]{2,1,0:T(8,128)} all-reduce(f32[1,32,64]{2,1,0:T(8,128)} %convolution_bitcast_fusion.8), channel_id=1, replica_groups=mesh['leaf'=8,'sub'=4] {'sub'}, use_global_device_ids=true, to_apply=%region_1.2 | all-reduce | flops 2048 | bytes 16384 | tf_op jit(solution)/shard_map/psum | solution.py:93
  307.4 33.0 %all_gather.7 = f32[8,32,64]{2,1,0:T(8,128)} all-gather(f32[1,32,64]{2,1,0:T(8,128)} %psum.15), channel_id=1, replica_groups=mesh['leaf'=8,'sub'=4] {'leaf'}, dimensions={0}, use_global_device_ids=true | all-gather | bytes 73728 | tf_op jit(solution)/shard_map/all_gather | solution.py:94
  342.5 6.6 %fusion.8 = f32[32,64,1]{1,0,2:T(8,128)S(1)} fusion(f32[6,32,64]{2,1,0:T(8,128)} %gather_fusion.8, f32[6]{0:T(128)} %copy-done.36, f32[]{:T(128)} %bitcast.28, f32[6,64]{1,0:T(8,128)S(1)} %get-tuple-element.58, f32[64]{0:T(128)} %copy-done.29, f32[]{:T(128)} %bitcast.25, f32[6,64]{1,0:T(8,128)} %copy-done.19, f32[64]{0:T(128)} %copy-done.30, f32[]{:T(128)} %bitcast.22, ...), kind=kOutput, calls=%fused_computation.40 | convolution fusion | flops 10346496 | bytes 71740 | tf_op jit(solution)/shard_map/krs,kps->pr/dot_general | solution.py:95
  353.2 10.4 %fusion.7 = f32[8,32,64,1]{2,1,3,0:T(8,128)S(1)} fusion(f32[8,32,64]{2,1,0:T(8,128)} %convolution_bitcast_fusion.4, f32[8,6,32,64]{3,2,1,0:T(8,128)} %bitcast.217, f32[8,6]{1,0:T(8,128)} %fusion.10, f32[]{:T(128)} %bitcast.28, f32[8,6,64]{2,1,0:T(8,128)} %get-tuple-element.66, f32[8,64]{1,0:T(8,128)S(1)} %bitcast.256, f32[]{:T(128)} %bitcast.25, ...), kind=kOutput, calls=%fused_computation.28 | convolution fusion | flops 82788352 | bytes 639204 | tf_op jit(solution)/shard_map/mkrs,mkps->mpr/dot_general | solution.py:89
  363.7 6.6 %convolution_convert_fusion = bf16[8,32,8,64]{3,1,2,0:T(8,128)(2,1)} fusion(f32[8,32,64,1]{2,1,3,0:T(8,128)S(1)} %fusion.7, f32[8,8,64,64]{3,2,1,0:T(8,128)S(1)} %bitcast.208), kind=kOutput, calls=%fused_computation.21 | convolution fusion | flops 100794368 | bytes 1376256 | tf_op jit(solution)/shard_map/mps,mcrs->mcpr/dot_general | solution.py:99
  370.2 2.7 pad_maximum_fusion.1
  373.0 4.6 %gather_fusion.6 = bf16[512,32,128]{2,1,0:T(8,128)(2,1)} fusion(bf16[192,32,128]{2,1,0:T(8,128)(2,1)} %pad_maximum_fusion.1, s32[1024]{0:T(1024)S(1)} %pad_clamp_fusion.2), kind=kCustom, calls=%fused_computation.6 | custom fusion | bytes 8390656 | tf_op jit(solution)/shard_map/gather | solution.py:106
  377.6 13.8 %fusion = f32[64,32,128]{2,1,0:T(8,128)} fusion(bf16[64,8,32,128]{3,2,1,0:T(8,128)(2,1)} %bitcast.209, bf16[64,32,128]{2,1,0:T(8,128)(2,1)} %fusion.2, f32[]{:T(128)} %bitcast.204, bf16[64,8,128,128]{3,2,1,0:T(8,128)(2,1)} %multiply_convert_fusion.5), kind=kOutput, calls=%fused_computation.15 | convolution fusion | flops 537657344 | bytes 22544388 | tf_op jit(solution)/shard_map/iknm,ikpm->ipn/dot_general | solution.py:103
  (142 shorter events, 51.1 us)
Async XLA Ops:
  0.6 22.8 %copy-start = (f32[64,64,64]{2,1,0:T(8,128)S(1)}, f32[64,64,64]{2,1,0:T(8,128)}, u32[]{:S(2)}) copy-start(f32[64,64,64]{2,1,0:T(8,128)} %param.16) | copy-start | bytes 3145732
  0.6 255.6 %collective-permute-start.1 = (bf16[64,32,128]{2,1,0:T(8,128)(2,1)}, bf16[64,32,128]{2,1,0:T(8,128)(2,1)}, u32[]{:S(2)}, u32[]{:S(2)}) collective-permute-start(bf16[64,32,128]{2,1,0:T(8,128)(2,1)} %param.14), channel_id=1, source_target_pairs={{1,0},{2,1},{3,2},{4,3},{5,4},{6,5},{7,6},{8,7},{9,8},{10,9},{11,1... | collective-permute-start | bytes 1572872 | tf_op jit(solution)/shard_map/ppermute | solution.py:17
  2.1 254.2 %collective-permute-start = (bf16[64,32,128]{2,1,0:T(8,128)(2,1)}, bf16[64,32,128]{2,1,0:T(8,128)(2,1)}, u32[]{:S(2)}, u32[]{:S(2)}) collective-permute-start(bf16[64,32,128]{2,1,0:T(8,128)(2,1)} %param.14), channel_id=1, source_target_pairs={{0,1},{1,2},{2,3},{3,4},{4,5},{5,6},{6,7},{7,8},{8,9},{9,10},{10,1... | collective-permute-start | bytes 1572872 | tf_op jit(solution)/shard_map/ppermute | solution.py:14
  5.9 79.3 %collective-permute-start.7 = (f32[8,8,64]{2,1,0:T(8,128)}, f32[8,8,64]{2,1,0:T(8,128)S(1)}, u32[]{:S(2)}, u32[]{:S(2)}) collective-permute-start(f32[8,8,64]{2,1,0:T(8,128)} %param.18), channel_id=1, source_target_pairs={{1,0},{2,1},{3,2},{4,3},{5,4},{6,5},{7,6},{8,7},{9,8},{10,9},{11,1... | collective-permute-start | bytes 49160 | tf_op jit(solution)/shard_map/ppermute | solution.py:17
  7.2 79.3 %collective-permute-start.6 = (f32[8,8,64]{2,1,0:T(8,128)}, f32[8,8,64]{2,1,0:T(8,128)S(1)}, u32[]{:S(2)}, u32[]{:S(2)}) collective-permute-start(f32[8,8,64]{2,1,0:T(8,128)} %param.18), channel_id=1, source_target_pairs={{0,1},{1,2},{2,3},{3,4},{4,5},{5,6},{6,7},{7,8},{8,9},{9,10},{10,1... | collective-permute-start | bytes 49160 | tf_op jit(solution)/shard_map/ppermute | solution.py:14
  11.6 103.8 %collective-permute-start.3 = (f32[64,8,128]{2,1,0:T(8,128)}, f32[64,8,128]{2,1,0:T(8,128)S(1)}, u32[]{:S(2)}, u32[]{:S(2)}) collective-permute-start(f32[64,8,128]{2,1,0:T(8,128)} %param.13), channel_id=1, source_target_pairs={{1,0},{2,1},{3,2},{4,3},{5,4},{6,5},{7,6},{8,7},{9,8},{10,9},{11,1... | collective-permute-start | bytes 786440 | tf_op jit(solution)/shard_map/ppermute | solution.py:17
  14.2 61.3 %copy-start.36 = (f32[6]{0:T(128)}, f32[6]{0:T(128)S(1)}, u32[]{:S(2)}) copy-start(f32[6]{0:T(128)S(1)} %fusion.12) | copy-start | bytes 76
  23.4 51.2 %copy-start.17 = (f32[8,8,64]{2,1,0:T(8,128)S(1)}, f32[8,8,64]{2,1,0:T(8,128)}, u32[]{:S(2)}) copy-start(f32[8,8,64]{2,1,0:T(8,128)} %param.19) | copy-start | bytes 49156
  24.9 57.7 %copy-start.18 = (s32[8,6]{1,0:T(8,128)S(1)}, s32[8,6]{1,0:T(8,128)}, u32[]{:S(2)}) copy-start(s32[8,6]{1,0:T(8,128)} %param.21) | copy-start | bytes 580
  24.9 58.3 %copy-start.7 = (f32[8,8,64]{2,1,0:T(8,128)S(1)}, f32[8,8,64]{2,1,0:T(8,128)}, u32[]{:S(2)}) copy-start(f32[8,8,64]{2,1,0:T(8,128)} %param.18) | copy-start | bytes 49156
  75.2 18.4 %copy-start.5 = (f32[64,8,128]{2,1,0:T(8,128)S(1)}, f32[64,8,128]{2,1,0:T(8,128)}, u32[]{:S(2)}) copy-start(f32[64,8,128]{2,1,0:T(8,128)} %param.13) | copy-start | bytes 786436
  75.3 14.9 %copy-start.28 = (f32[64]{0:T(128)}, f32[64]{0:T(128)S(1)}, u32[]{:S(2)}) copy-start(f32[64]{0:T(128)S(1)} %get-tuple-element.42) | copy-start | bytes 772
  75.3 14.9 %copy-start.29 = (f32[64]{0:T(128)}, f32[64]{0:T(128)S(1)}, u32[]{:S(2)}) copy-start(f32[64]{0:T(128)S(1)} %get-tuple-element.43) | copy-start | bytes 772
  75.3 14.9 %copy-start.30 = (f32[64]{0:T(128)}, f32[64]{0:T(128)S(1)}, u32[]{:S(2)}) copy-start(f32[64]{0:T(128)S(1)} %get-tuple-element.44) | copy-start | bytes 772
  75.3 14.9 %copy-start.31 = (f32[64]{0:T(128)}, f32[64]{0:T(128)S(1)}, u32[]{:S(2)}) copy-start(f32[64]{0:T(128)S(1)} %get-tuple-element.45) | copy-start | bytes 772
  85.2 8.4 %collective-permute-start.5 = (f32[8,32,64]{2,1,0:T(8,128)S(1)}, f32[8,32,64]{2,1,0:T(8,128)}, u32[]{:S(2)}, u32[]{:S(2)}) collective-permute-start(f32[8,32,64]{2,1,0:T(8,128)S(1)} %convolution_bitcast_fusion.7), channel_id=1, source_target_pairs={{1,0},{2,1},{3,2},{4,3},{5,4},{6,5},{7,6},{8,7},{9,8},{10,9},{11,1... | collective-permute-start | bytes 196616 | tf_op jit(solution)/shard_map/ppermute | solution.py:17
  86.5 9.2 %collective-permute-start.4 = (f32[8,32,64]{2,1,0:T(8,128)S(1)}, f32[8,32,64]{2,1,0:T(8,128)}, u32[]{:S(2)}, u32[]{:S(2)}) collective-permute-start(f32[8,32,64]{2,1,0:T(8,128)S(1)} %convolution_bitcast_fusion.7), channel_id=1, source_target_pairs={{0,1},{1,2},{2,3},{3,4},{4,5},{5,6},{6,7},{7,8},{8,9},{9,10},{10,1... | collective-permute-start | bytes 196616 | tf_op jit(solution)/shard_map/ppermute | solution.py:14
  93.5 22.5 %collective-permute-start.2 = (f32[64,8,128]{2,1,0:T(8,128)S(1)}, f32[64,8,128]{2,1,0:T(8,128)}, u32[]{:S(2)}, u32[]{:S(2)}) collective-permute-start(f32[64,8,128]{2,1,0:T(8,128)S(1)} %copy-done.5), channel_id=1, source_target_pairs={{0,1},{1,2},{2,3},{3,4},{4,5},{5,6},{6,7},{7,8},{8,9},{9,10},{10,1... | collective-permute-start | bytes 786440 | tf_op jit(solution)/shard_map/ppermute | solution.py:14
  192.4 63.9 %copy-start.2 = (bf16[64,32,128]{2,1,0:T(8,128)(2,1)S(1)}, bf16[64,32,128]{2,1,0:T(8,128)(2,1)}, u32[]{:S(2)}) copy-start(bf16[64,32,128]{2,1,0:T(8,128)(2,1)} %param.14) | copy-start | bytes 1572868
  279.9 90.3 %collective-permute-start.9 = (bf16[64,32,128]{2,1,0:T(8,128)(2,1)}, bf16[64,32,128]{2,1,0:T(8,128)(2,1)}, u32[]{:S(2)}, u32[]{:S(2)}) collective-permute-start(bf16[64,32,128]{2,1,0:T(8,128)(2,1)} %fusion.2), channel_id=1, source_target_pairs={{1,0},{2,1},{3,2},{4,3},{5,4},{6,5},{7,6},{8,7},{9,8},{10,9},{11,1... | collective-permute-start | bytes 1572872 | tf_op jit(solution)/shard_map/ppermute | solution.py:17
  281.2 89.0 %collective-permute-start.8 = (bf16[64,32,128]{2,1,0:T(8,128)(2,1)}, bf16[64,32,128]{2,1,0:T(8,128)(2,1)}, u32[]{:S(2)}, u32[]{:S(2)}) collective-permute-start(bf16[64,32,128]{2,1,0:T(8,128)(2,1)} %fusion.2), channel_id=1, source_target_pairs={{0,1},{1,2},{2,3},{3,4},{4,5},{5,6},{6,7},{7,8},{8,9},{9,10},{10,1... | collective-permute-start | bytes 1572872 | tf_op jit(solution)/shard_map/ppermute | solution.py:14
  288.1 62.5 %copy-start.4 = (f32[8,32,64]{2,1,0:T(8,128)}, f32[8,32,64]{2,1,0:T(8,128)S(1)}, u32[]{:S(2)}) copy-start(f32[8,32,64]{2,1,0:T(8,128)S(1)} %convolution_bitcast_fusion.5) | copy-start | bytes 196612
  289.1 61.6 %collective-permute-start.11 = (f32[8,32,64]{2,1,0:T(8,128)S(1)}, f32[8,32,64]{2,1,0:T(8,128)}, u32[]{:S(2)}, u32[]{:S(2)}) collective-permute-start(f32[8,32,64]{2,1,0:T(8,128)S(1)} %convolution_bitcast_fusion.5), channel_id=1, source_target_pairs={{1,0},{2,1},{3,2},{4,3},{5,4},{6,5},{7,6},{8,7},{9,8},{10,9},{11,1... | collective-permute-start | bytes 196616 | tf_op jit(solution)/shard_map/ppermute | solution.py:17
  290.3 60.3 %collective-permute-start.10 = (f32[8,32,64]{2,1,0:T(8,128)S(1)}, f32[8,32,64]{2,1,0:T(8,128)}, u32[]{:S(2)}, u32[]{:S(2)}) collective-permute-start(f32[8,32,64]{2,1,0:T(8,128)S(1)} %convolution_bitcast_fusion.5), channel_id=1, source_target_pairs={{0,1},{1,2},{2,3},{3,4},{4,5},{5,6},{6,7},{7,8},{8,9},{9,10},{10,1... | collective-permute-start | bytes 196616 | tf_op jit(solution)/shard_map/ppermute | solution.py:14
  (25 other events, 182.3 us)
where the time goes:
time: 400 us; the launch traced here: 394 us
  other arithmetic  139 us (35%)
  blocking collectives  95.2 us (24%)
  matrix products  89.1 us (22%)
  local copies, waits for them, and re-layouts  38.4 us (10%)
  starting transfers between devices  29.4 us (7%)
    dot_general x2, other arithmetic, on_device(): jnp.einsum('iknm,ikpm->ipn', near_blocks, wide_vector[near_local], prefer...  127 us
    all_gather x2, blocking collectives, on_device(): all_top = lax.all_gather(group_total[None], 'leaf', axis=0, tiled=True)  66.6 us
    psum x2, blocking collectives, on_device(): group_total = lax.psum(partial_top, 'sub')  28.6 us
    dot_general x2, matrix products, on_device(): jnp.einsum('iknm,ikpm->ipn', near_blocks, wide_vector[near_local], prefer...  27.7 us
    ppermute x6, starting transfers between devices, padded(): lax.ppermute(lax.slice_in_dim(block, block.shape[dim] - width, None, axis...  21.6 us
    dot_general x2, matrix products, on_device(): jnp.einsum('mkrs,mkps->mpr', mid_coupling, wide_coef[mid_local_ids], prec...  20.9 us
    dot_general x2, matrix products, on_device(): jnp.einsum('mps,mcrs->mcpr', mid_total, transfer_groups, precision=highest)  13.1 us
    dot_general x2, matrix products, on_device(): jnp.einsum('krs,kps->pr', top_coupling, all_top[top_clipped], precision=h...  12.3 us
  transfers between devices with their start and end apart: 12, of which 0 were waited for; matrix products, arithmetic and copies ran while one was open for 55% of the time, Pallas kernels for 0%

commit v1 on v0

v1 whole, which is shorter than its diff:
```python
import functools
import math

import jax
import jax.numpy as jnp
from jax import lax
from jax.experimental import pallas as pl
from jax.experimental.pallas import tpu as pltpu
from jax.sharding import PartitionSpec as P

MATVECS = 2
AXES = ("leaf", "sub")
F32 = jnp.float32
BF16 = jnp.bfloat16
HIGHEST = lax.Precision.HIGHEST
LN2 = math.log(2.0)
DISTANCE_SCALE = math.sqrt(3.0) / LN2
MIB = 1 << 20

VMEM = pl.BlockSpec(memory_space=pltpu.VMEM)
SMEM = pl.BlockSpec(memory_space=pltpu.SMEM)


def split(value):
    high = value.astype(BF16).astype(F32)
    rest = value - high
    mid = rest.astype(BF16).astype(F32)
    low = (rest - mid).astype(BF16).astype(F32)
    return high, mid, low


def features(points, scale):
    scaled = points * scale
    high, mid, low = split(scaled)
    norm = jnp.sum(scaled * scaled, axis=0, keepdims=True)
    norm_high, norm_mid, norm_low = split(norm)
    row = lax.broadcasted_iota(jnp.int32, points.shape, 0)
    one = jnp.ones_like(norm)

    def rows(values):
        block = jnp.zeros_like(points)
        for index, value in enumerate(values):
            block = jnp.where(row == index, value, block)
        return block

    norms = (norm_high, norm_mid, norm_low)
    ones = (one, one, one)
    pad = jnp.zeros_like(points)
    left = jnp.concatenate([high, high, mid, mid, high, low, rows(norms + ones), pad], axis=0)
    right = jnp.concatenate(
        [-2.0 * x for x in (high, mid, high, mid, low, high)] + [rows(ones + norms), pad], axis=0
    )
    return left, right


def kernel_of(squared, amp):
    squared = jnp.maximum(squared, 1e-20)
    root = squared * lax.rsqrt(squared)
    return (amp + (amp * LN2) * root) * jnp.exp2(-root)


def dot(a, b, precision=None):
    return jnp.dot(a, b, preferred_element_type=F32, precision=precision)


def dot_nt(a, b):
    return lax.dot_general(a, b, (((1,), (1,)), ((), ())), preferred_element_type=F32)


def call(body, outs, in_specs, scratch=(), limit=24, cost=0, aliases=None, name=None, out_specs=None):
    return pl.pallas_call(
        body,
        out_shape=outs,
        in_specs=in_specs,
        out_specs=out_specs if out_specs is not None else [VMEM] * len(outs),
        scratch_shapes=list(scratch),
        input_output_aliases=aliases or {},
        compiler_params=pltpu.CompilerParams(vmem_limit_bytes=limit * MIB),
        cost_estimate=pl.CostEstimate(flops=cost, bytes_accessed=cost // 16, transcendentals=0),
        name=name,
    )


def near_items(order, slots, column, left, right, blocks, amp, start, count, group, near):
    def step(turn, carry):
        for inner in range(group):
            item = start + jnp.minimum(turn * group + inner, count - 1)
            slot = order[item]
            squared = dot(left[column(slots[slot])], right[lax.div(slot, near)])
            blocks[slot] = kernel_of(squared, amp).astype(BF16)
        return carry

    lax.fori_loop(0, lax.div(count + group - 1, group), step, 0)


def store_features(points, scale, left, right, base, count, unroll):
    def step(turn, carry):
        for inner in range(unroll):
            leaf = turn * unroll + inner
            left_block, right_block = features(points[leaf], scale)
            left[base + leaf] = left_block.T.astype(BF16)
            if right is not None:
                right[leaf] = right_block.astype(BF16)
        return carry

    lax.fori_loop(0, count // unroll, step, 0)


def local_body(near, order, slots, counts, amp, points, scale, blocks, right, left):
    leaves = points.shape[0]
    store_features(points, scale[...], left, right, 0, leaves, 4)
    near_items(
        order, slots, lambda j: j - leaves, left, right, blocks, amp[0], 0, counts[0], 4, near
    )


def halo_body(near, order, slots, counts, amp, low, high, scale, right, blocks_in, blocks, left):
    leaves = low.shape[0]
    store_features(low, scale[...], left, None, 0, leaves, 4)
    store_features(high, scale[...], left, None, leaves, leaves, 4)

    def column(j):
        return jnp.where(j < leaves, j, j - leaves)

    near_items(order, slots, column, left, right, blocks, amp[0], counts[0], counts[1], 4, near)
    empty = jnp.zeros(blocks.shape[1:], BF16)

    def clear(item, carry):
        blocks[order[item]] = empty
        return carry

    lax.fori_loop(counts[0] + counts[1], blocks.shape[0], clear, 0)


def up_group(vector, operator, group, members):
    total = None
    for member in range(members):
        leaf = group * members + member
        term = dot_nt(vector(leaf), operator[leaf])
        total = term if total is None else total + term
    rank = total.shape[1] // 2
    return total[:, :rank] + total[:, rank:]


def prepare_body(members, probes, basis, transfer, top_transfer, skeleton, operator, mid, top):
    rank = basis.shape[1]
    groups = mid.shape[0]
    probe_count = probes.shape[1]

    def step(group, total):
        for member in range(members):
            leaf = group * members + member
            matrix = transfer[leaf]
            high = matrix.astype(BF16)
            low = (matrix - high.astype(F32)).astype(BF16)
            both = jnp.concatenate([high.astype(F32), low.astype(F32)], axis=1).T.astype(BF16)
            product = dot(both, basis[leaf])
            folded = product[:rank] + product[rank:]
            upper = folded.astype(BF16)
            operator[leaf, :rank] = upper
            operator[leaf, rank:] = (folded - upper.astype(F32)).astype(BF16)
        coef = up_group(lambda leaf: probes[leaf], operator, group, members)
        mid[group, :probe_count] = coef
        mid[group, probe_count:] = skeleton[group]
        return total + dot(coef, top_transfer[group], HIGHEST)

    top[...] = lax.fori_loop(0, groups, step, jnp.zeros(top.shape, F32))


def skeleton_body(
    probe_count, entries, mid_ids, mid_on, top_ids, top_on, place, amp, own, low, high, tops, scale, mid_out, top_out, left, right
):
    groups = own.shape[0]
    scale = scale[...][:, : own.shape[2]]

    def store(source, base, keep_right):
        def step(group, carry):
            a, b = features(source[group, probe_count:], scale)
            left[base + group] = a.T.astype(BF16)
            if keep_right:
                right[group] = b.astype(BF16)
            return carry

        lax.fori_loop(0, groups, step, 0)

    store(low, 0, False)
    store(own, groups, True)
    store(high, 2 * groups, False)

    def mid_step(group, carry):
        for entry in range(entries):
            item = group * entries + entry
            value = kernel_of(dot(left[mid_ids[item]], right[group]), amp[0])
            mid_out[item] = jnp.where(mid_on[item] > 0, value, 0.0)
        return carry

    lax.fori_loop(0, groups, mid_step, 0)
    _, mine = features(tops[place[0]], scale)
    mine = mine.astype(BF16)
    for entry in range(top_out.shape[0]):
        other, _ = features(tops[top_ids[entry]], scale)
        value = kernel_of(dot(other.T.astype(BF16), mine), amp[0])
        top_out[entry] = jnp.where(top_on[entry] > 0, value, 0.0)


def middle_body(
    probe_count, entries, mid_ids, top_slots, own, low, high, tops, mid_coupling, top_coupling, top_transfer, total, table
):
    groups = own.shape[0]

    def fill(group, carry):
        table[group] = low[group, :probe_count]
        table[groups + group] = own[group, :probe_count]
        table[2 * groups + group] = high[group, :probe_count]
        return carry

    lax.fori_loop(0, groups, fill, 0)
    top_local = None
    for entry in range(top_coupling.shape[0]):
        term = dot(tops[top_slots[entry]], top_coupling[entry], HIGHEST)
        top_local = term if top_local is None else top_local + term

    def step(group, carry):
        value = lax.dot_general(
            top_local,
            top_transfer[group],
            (((1,), (1,)), ((), ())),
            preferred_element_type=F32,
            precision=HIGHEST,
        )
        for entry in range(entries):
            item = group * entries + entry
            value = value + dot(table[mid_ids[item]], mid_coupling[item], HIGHEST)
        total[group] = value
        return carry

    lax.fori_loop(0, groups, step, 0)


def product_body(members, near, again, slots, noise, low, own, high, blocks, operator, total, top_transfer, *rest):
    if again:
        out, mid, top, table = rest
    else:
        out, table = rest
    leaves, probe_count = own.shape[0], own.shape[1]
    rank = total.shape[2]
    points = own.shape[2]

    def fill(leaf, carry):
        table[leaf] = low[leaf]
        table[leaves + leaf] = own[leaf]
        table[2 * leaves + leaf] = high[leaf]
        return carry

    lax.fori_loop(0, leaves, fill, 0, unroll=4)

    def step(group, carry):
        local = total[group]
        upper = local.astype(BF16)
        lower = (local - upper.astype(F32)).astype(BF16)
        twice = jnp.concatenate([upper, upper], axis=1)
        for member in range(members):
            leaf = group * members + member
            gathered = jnp.concatenate(
                [table[slots[leaf * near + entry]] for entry in range(near)], axis=1
            )
            weights = blocks[pl.ds(leaf * near, near)].reshape(near * points, points)
            value = dot(gathered, weights)
            value = value + dot(twice, operator[leaf]) + dot(lower, operator[leaf, :rank])
            value = value + noise[0] * own[leaf].astype(F32)
            out[leaf] = value.astype(BF16)
        if again:
            coef = up_group(lambda leaf: out[leaf], operator, group, members)
            mid[group] = coef
            carry = carry + dot(coef, top_transfer[group], HIGHEST)
        return carry

    groups = total.shape[0]
    result = lax.fori_loop(0, groups, step, jnp.zeros((probe_count, rank), F32))
    if again:
        top[...] = result


def neighbours(block):
    count = lax.axis_size(AXES)
    forward = [(i, i + 1) for i in range(count - 1)]
    backward = [(target, source) for source, target in forward]
    return lax.ppermute(block, AXES, forward), lax.ppermute(block, AXES, backward)


def top_exchange(partial):
    size = lax.axis_size("sub")
    step = 1
    while step < size:
        partial = partial + lax.ppermute(partial, "sub", [(i, i ^ step) for i in range(size)])
        step *= 2
    blocks = partial[None]
    size = lax.axis_size("leaf")
    step = 1
    while step < size:
        other = lax.ppermute(blocks, "leaf", [(i, i ^ step) for i in range(size)])
        blocks = jnp.concatenate([blocks, other], axis=0)
        step *= 2
    return blocks


def work_list(kind):
    count = kind.shape[0]
    item = jnp.arange(count, dtype=jnp.int32)
    before = (kind[:, None] > kind[None, :]) | (
        (kind[:, None] == kind[None, :]) & (item[:, None] > item[None, :])
    )
    place = jnp.sum(before.astype(jnp.int32), axis=1)
    order = jnp.sum(jnp.where(place[:, None] == item[None, :], item[:, None], 0), axis=0)
    counts = jnp.stack([jnp.sum((kind == which).astype(jnp.int32)) for which in range(2)])
    return order, counts


def on_device(
    points,
    probes,
    leaf_basis,
    mid_transfer,
    top_transfer,
    mid_skeleton,
    top_skeleton,
    near_list,
    mid_list,
    top_list,
    inv_scale,
    amplitude,
    noise_var,
):
    leaves, feat, size = points.shape
    groups, _, rank = mid_skeleton.shape
    probe_count = probes.shape[1]
    members = leaves // groups
    near = near_list.shape[1]
    entries = mid_list.shape[1]
    position = lax.axis_index("leaf") * lax.axis_size("sub") + lax.axis_index("sub")
    top_index = lax.axis_index("leaf")

    low_points, high_points = neighbours(points)
    low_probes, high_probes = neighbours(probes)

    flat = near_list.reshape(-1)
    present = flat >= 0
    slots = jnp.where(present, flat - position * leaves + leaves, leaves)
    outside = (slots < leaves) | (slots >= 2 * leaves)
    kind = jnp.where(present, outside.astype(jnp.int32), 2)
    order, counts = work_list(kind)
    scale = jnp.broadcast_to((inv_scale * DISTANCE_SCALE)[:, None], (feat, size))

    mid_flat = mid_list.reshape(-1)
    mid_on = (mid_flat >= 0).astype(jnp.int32)
    mid_ids = jnp.where(mid_flat >= 0, mid_flat - position * groups + groups, groups)
    top_row = top_list.reshape(-1)
    top_on = (top_row >= 0).astype(jnp.int32)
    top_ids = jnp.where(top_row >= 0, top_row, 0)
    top_slots = jnp.where(top_row >= 0, top_row ^ top_index, 0)
    place = top_index.reshape(1).astype(jnp.int32)

    sds = jax.ShapeDtypeStruct
    operator, mid, top = call(
        functools.partial(prepare_body, members),
        [
            sds((leaves, 2 * rank, size), BF16),
            sds((groups, probe_count + feat, rank), F32),
            sds((probe_count, rank), F32),
        ],
        [VMEM] * 5,
        name="prepare",
        cost=2 * leaves * rank * rank * size * 2,
    )(probes, leaf_basis, mid_transfer, top_transfer, mid_skeleton)

    blocks, right = call(
        functools.partial(local_body, near),
        [sds((leaves * near, size, size), BF16), sds((leaves, 8 * feat, size), BF16)],
        [SMEM] * 4 + [VMEM] * 2,
        scratch=[pltpu.VMEM((leaves, size, 8 * feat), BF16)],
        name="near_local",
        cost=leaves * near * size * size * 40,
    )(order, slots, counts, amplitude, points, scale)

    blocks = call(
        functools.partial(halo_body, near),
        [sds((leaves * near, size, size), BF16)],
        [SMEM] * 4 + [VMEM] * 5,
        scratch=[pltpu.VMEM((2 * leaves, size, 8 * feat), BF16)],
        aliases={8: 0},
        name="near_halo",
        cost=leaves * near * size * size * 40,
    )(order, slots, counts, amplitude, low_points, high_points, scale, right, blocks)[0]

    mid_coupling = top_coupling = None
    vector, low, high = probes, low_probes, high_probes
    results = []
    for turn in range(MATVECS):
        if turn > 0:
            low, high = neighbours(vector)
        low_mid, high_mid = neighbours(mid)
        tops = top_exchange(top)
        if turn == 0:
            mid_coupling, top_coupling = call(
                functools.partial(skeleton_body, probe_count, entries),
                [
                    sds((groups * entries, rank, rank), F32),
                    sds((top_row.shape[0], rank, rank), F32),
                ],
                [SMEM] * 6 + [VMEM] * 5,
                scratch=[
                    pltpu.VMEM((3 * groups, rank, 8 * feat), BF16),
                    pltpu.VMEM((groups, 8 * feat, rank), BF16),
                ],
                name="skeleton",
                cost=groups * entries * rank * rank * 40,
            )(
                mid_ids, mid_on, top_ids, top_on, place, amplitude,
                mid, low_mid, high_mid, top_skeleton, scale,
            )
        total = call(
            functools.partial(middle_body, probe_count, entries),
            [sds((groups, probe_count, rank), F32)],
            [SMEM] * 2 + [VMEM] * 7,
            scratch=[pltpu.VMEM((3 * groups, probe_count, rank), F32)],
            name="middle",
            cost=groups * entries * rank * rank * probe_count * 12,
        )(
            mid_ids, top_slots, mid, low_mid, high_mid, tops,
            mid_coupling, top_coupling, top_transfer,
        )[0]
        again = turn + 1 < MATVECS
        outs = [sds(vector.shape, BF16)]
        if again:
            outs += [sds((groups, probe_count, rank), F32), sds((probe_count, rank), F32)]
        values = call(
            functools.partial(product_body, members, near, again),
            outs,
            [SMEM] * 2 + [VMEM] * 7,
            scratch=[pltpu.VMEM((3 * leaves, probe_count, size), BF16)],
            name="product",
            cost=2 * leaves * near * size * size * probe_count,
        )(slots, noise_var, low, vector, high, blocks, operator, total, top_transfer)
        vector = values[0]
        results.append(vector)
        if again:
            mid, top = values[1], values[2]
    return (results[0], results[1])


def solution(mesh):
    whole = P(AXES, None, None)
    in_specs = (
        whole, whole, whole, whole, whole, whole,
        P(), P(AXES, None), P(AXES, None), P("leaf", None), P(), P(), P(),
    )
    return jax.shard_map(
        on_device, mesh=mesh, in_specs=in_specs, out_specs=(whole, whole), check_vma=False
    )
```

time: 400 us -> 156 us (0.39)
  the two profiles are of different devices: /device:TPU:0 before, /device:TPU:7 now
where the time goes in v1:
time: 156 us; the launch traced here: 155 us
  Pallas kernels  66.9 us (43%)
  starting transfers between devices  49.9 us (32%)
  waiting for transfers between devices  22.7 us (15%)
  local copies, waits for them, and re-layouts  8.41 us (5%)
  other arithmetic  4.56 us (3%)
  between operations  2.33 us (1%)
    ppermute x5, starting transfers between devices, neighbours(): lax.ppermute(block, AXES, forward)  29.6 us
    pallas_call x1, Pallas kernels, on_device(): call(functools.partial(local_body, near), [sds((leaves * near, size, size...  16.6 us
    pallas_call x1, Pallas kernels, on_device(): call(functools.partial(halo_body, near), [sds((leaves * near, size, size)...  15.7 us
    pallas_call x2, Pallas kernels, on_device(): call(functools.partial(product_body, members, near, again), outs, [SMEM]...  15.3 us
    ppermute x5, waiting for transfers between devices, neighbours(): lax.ppermute(block, AXES, backward)  11.8 us
    ppermute x5, starting transfers between devices, neighbours(): lax.ppermute(block, AXES, backward)  9.83 us
    ppermute x6, starting transfers between devices, top_exchange(): other = lax.ppermute(blocks, 'leaf', [(i, i ^ step) for i in range(size)])  9.49 us
    ppermute x6, waiting for transfers between devices, top_exchange(): other = lax.ppermute(blocks, 'leaf', [(i, i ^ step) for i in range(size)])  8 us
  transfers between devices with their start and end apart: 20, of which 9 were waited for; matrix products, arithmetic and copies ran while one was open for 4% of the time, Pallas kernels for 33%

profile of v1, /device:TPU:7, one launch (start us, length us, event | category | flops | bytes accessed | tf_op | source)
XLA Modules:
  0.0 154.7 jit_solution(1539463323470906972)
XLA Ops:
  0.6 3.7 %collective-permute-start = (bf16[64,32,128]{2,1,0:T(8,128)(2,1)}, bf16[64,32,128]{2,1,0:T(8,128)(2,1)S(1)}, u32[]{:S(2)}, u32[]{:S(2)}) collective-permute-start(bf16[64,32,128]{2,1,0:T(8,128)(2,1)} %own.1), channel_id=1, source_target_pairs={{0,1},{1,2},{2,3},{3,4},{4,5},{5,6},{6,7},{7,8},{8,9},{9,10},{10,1... | collective-permute-start | bytes 1572872 | tf_op jit(solution)/shard_map/ppermute | solution.py:288
  4.3 1.9 %collective-permute-start.1 = (bf16[64,32,128]{2,1,0:T(8,128)(2,1)}, bf16[64,32,128]{2,1,0:T(8,128)(2,1)}, u32[]{:S(2)}, u32[]{:S(2)}) collective-permute-start(bf16[64,32,128]{2,1,0:T(8,128)(2,1)} %own.1), channel_id=1, source_target_pairs={{1,0},{2,1},{3,2},{4,3},{5,4},{6,5},{7,6},{8,7},{9,8},{10,9},{11,1... | collective-permute-start | bytes 1572872 | tf_op jit(solution)/shard_map/ppermute | solution.py:288
  6.3 5.4 %collective-permute-start.2 = (f32[64,8,128]{2,1,0:T(8,128)}, f32[64,8,128]{2,1,0:T(8,128)S(1)}, u32[]{:S(2)}, u32[]{:S(2)}) collective-permute-start(f32[64,8,128]{2,1,0:T(8,128)} %points.1), channel_id=1, source_target_pairs={{0,1},{1,2},{2,3},{3,4},{4,5},{5,6},{6,7},{7,8},{8,9},{9,10},{10,1... | collective-permute-start | bytes 786440 | tf_op jit(solution)/shard_map/ppermute | solution.py:288
  11.7 1.9 %collective-permute-start.3 = (f32[64,8,128]{2,1,0:T(8,128)}, f32[64,8,128]{2,1,0:T(8,128)}, u32[]{:S(2)}, u32[]{:S(2)}) collective-permute-start(f32[64,8,128]{2,1,0:T(8,128)} %points.1), channel_id=1, source_target_pairs={{1,0},{2,1},{3,2},{4,3},{5,4},{6,5},{7,6},{8,7},{9,8},{10,9},{11,1... | collective-permute-start | bytes 786440 | tf_op jit(solution)/shard_map/ppermute | solution.py:288
  19.2 7.4 %prepare.1 = (bf16[64,128,128]{2,1,0:T(8,128)(2,1)S(1)}, f32[8,40,64]{2,1,0:T(8,128)S(1)}, f32[32,64]{1,0:T(8,128)S(1)}) custom-call(bf16[64,32,128]{2,1,0:T(8,128)(2,1)S(1)} %copy-done.2, bf16[64,64,128]{2,1,0:T(8,128)(2,1)S(1)} %copy-done.5, f32[64,64,64]{2,1,0:T(8,128)S(1)} %copy-done.4, f32[8,64,64]{2,1,0:T(8,128)S(1)} %copy-done, f32[8,8,64]{2,1,0:T(8,128)S(1)} %copy-done.7), custom_call_target="tpu_custom_call" | custom-call | flops 134217728 | bytes 8388608 | tf_op jit(solution)/shard_map/prepare/pallas_call | solution.py:364
  31.6 2.1 %collective-permute-done.8 = f32[1,32,64]{2,1,0:T(8,128)S(1)} collective-permute-done((f32[1,32,64]{2,1,0:T(8,128)S(1)}, f32[1,32,64]{2,1,0:T(8,128)S(1)}, u32[]{:S(2)}, u32[]{:S(2)}) %collective-permute-start.8) | collective-permute-done | bytes 8224 | tf_op jit(solution)/shard_map/ppermute | solution.py:301
  36.5 2.4 %collective-permute-start.10 = (f32[4,32,64]{2,1,0:T(8,128)S(1)}, f32[4,32,64]{2,1,0:T(8,128)S(1)}, u32[]{:S(2)}, u32[]{:S(2)}) collective-permute-start(f32[4,32,64]{2,1,0:T(8,128)S(1)} %pad_maximum_fusion.2), channel_id=1, source_target_pairs={{0,16},{4,20},{8,24},{12,28},{16,0},{20,4},{24,8},{28,12},{1,17},{... | collective-permute-start | bytes 98312 | tf_op jit(solution)/shard_map/ppermute | solution.py:301
  40.6 10.0 %collective-permute-start.4 = (f32[8,40,64]{2,1,0:T(8,128)S(1)}, f32[8,40,64]{2,1,0:T(8,128)S(1)}, u32[]{:S(2)}, u32[]{:S(2)}) collective-permute-start(f32[8,40,64]{2,1,0:T(8,128)S(1)} %get-tuple-element.15.own), channel_id=1, source_target_pairs={{0,1},{1,2},{2,3},{3,4},{4,5},{5,6},{6,7},{7,8},{8,9},{9,10},{10,1... | collective-permute-start | bytes 245768 | tf_op jit(solution)/shard_map/ppermute | solution.py:288
  55.7 16.6 %near_local.1 = (bf16[512,128,128]{2,1,0:T(8,128)(2,1)S(1)}, bf16[64,64,128]{2,1,0:T(8,128)(2,1)S(1)}) custom-call(s32[512]{0:T(512)S(1)} %select_reduce_fusion.order, s32[512]{0:T(512)S(1)} %get-tuple-element.27.slots, s32[2]{0:T(128)S(1)} %pad_add_fusion.counts, f32[1]{0:T(128)S(6)} %copy.21.amp, f32[64,8,128]{2,1,0:T(8,128)S(1)} %copy-done.9, ...), custom_call_target="tpu_custom_call" | custom-call | flops 335544320 | bytes 20971520 | tf_op jit(solution)/shard_map/near_local/pallas_call | solution.py:376
  72.4 1.9 %collective-permute-start.5 = (f32[8,40,64]{2,1,0:T(8,128)S(1)}, f32[8,40,64]{2,1,0:T(8,128)S(1)}, u32[]{:S(2)}, u32[]{:S(2)}) collective-permute-start(f32[8,40,64]{2,1,0:T(8,128)S(1)} %get-tuple-element.15.own), channel_id=1, source_target_pairs={{1,0},{2,1},{3,2},{4,3},{5,4},{6,5},{7,6},{8,7},{9,8},{10,9},{11,1... | collective-permute-start | bytes 245768 | tf_op jit(solution)/shard_map/ppermute | solution.py:288
  75.2 5.6 %collective-permute-done.5.high = f32[8,40,64]{2,1,0:T(8,128)S(1)} collective-permute-done((f32[8,40,64]{2,1,0:T(8,128)S(1)}, f32[8,40,64]{2,1,0:T(8,128)S(1)}, u32[]{:S(2)}, u32[]{:S(2)}) %collective-permute-start.5) | collective-permute-done | bytes 81952 | tf_op jit(solution)/shard_map/ppermute | solution.py:288
  80.8 4.7 %skeleton.3 = (f32[48,64,64]{2,1,0:T(8,128)S(1)}, f32[6,64,64]{2,1,0:T(8,128)S(1)}) custom-call(s32[48]{0:T(128)S(1)} %select_n.44.mid_ids, s32[48]{0:T(128)S(1)} %reshape.64.mid_on, s32[6]{0:T(128)S(1)} %get-tuple-element.28.top_ids, s32[6]{0:T(128)S(1)} %compare_convert_fusion.top_on, s32[1]{0:T(128)} %bitcast.4.place, f32[1]{0:T(128)S(6)} %copy.21.amp, ...), custom_call_target="tpu_custom_call" | custom-call | flops 7864320 | bytes 491520 | tf_op jit(solution)/shard_map/skeleton/pallas_call | solution.py:404
  85.5 3.6 %middle.2.total = f32[8,32,64]{2,1,0:T(8,128)S(1)} custom-call(s32[48]{0:T(128)S(1)} %select_n.44.mid_ids, s32[6]{0:T(128)S(1)} %get-tuple-element.29.top_slots, f32[8,40,64]{2,1,0:T(8,128)S(1)} %get-tuple-element.15.own, f32[8,40,64]{2,1,0:T(8,128)S(1)} %collective-permute-done.4.low, f32[8,40,64]{2,1,0:T(8,128)S(1)} %collective-permute-done.5.high, ...), custom_call_target="tpu_custom_call" | custom-call | flops 75497472 | bytes 4718592 | tf_op jit(solution)/shard_map/middle/pallas_call | solution.py:421
  89.1 15.7 %near_halo.1.blocks = bf16[512,128,128]{2,1,0:T(8,128)(2,1)S(1)} custom-call(s32[512]{0:T(512)S(1)} %select_reduce_fusion.order, s32[512]{0:T(512)S(1)} %get-tuple-element.27.slots, s32[2]{0:T(128)S(1)} %pad_add_fusion.counts, f32[1]{0:T(128)S(6)} %copy.21.amp, f32[64,8,128]{2,1,0:T(8,128)S(1)} %collective-permute-done.2.low, ...), custom_call_target="tpu_custom_call", output_to_operand_aliasing={{}: (8, {})} | custom-call | flops 335544320 | bytes 20971520 | tf_op jit(solution)/shard_map/near_halo/pallas_call | solution.py:385
  104.9 9.3 %product.2 = (bf16[64,32,128]{2,1,0:T(8,128)(2,1)}, f32[8,32,64]{2,1,0:T(8,128)S(1)}, f32[32,64]{1,0:T(8,128)S(1)}) custom-call(s32[512]{0:T(512)S(1)} %get-tuple-element.27.slots, f32[1]{0:T(128)S(6)} %copy.22.noise, bf16[64,32,128]{2,1,0:T(8,128)(2,1)S(1)} %collective-permute-done.low, bf16[64,32,128]{2,1,0:T(8,128)(2,1)S(1)} %copy-done.3, ...), custom_call_target="tpu_custom_call" | custom-call | flops 536870912 | bytes 33554432 | tf_op jit(solution)/shard_map/product/pallas_call | solution.py:436
  115.3 2.2 %collective-permute-start.11 = (bf16[64,32,128]{2,1,0:T(8,128)(2,1)}, bf16[64,32,128]{2,1,0:T(8,128)(2,1)S(1)}, u32[]{:S(2)}, u32[]{:S(2)}) collective-permute-start(bf16[64,32,128]{2,1,0:T(8,128)(2,1)} %get-tuple-element.10.own), channel_id=1, source_target_pairs={{0,1},{1,2},{2,3},{3,4},{4,5},{5,6},{6,7},{7,8},{8,9},{9,10},{10,1... | collective-permute-start | bytes 1572872 | tf_op jit(solution)/shard_map/ppermute | solution.py:288
  117.5 2.1 %collective-permute-start.12 = (bf16[64,32,128]{2,1,0:T(8,128)(2,1)}, bf16[64,32,128]{2,1,0:T(8,128)(2,1)S(1)}, u32[]{:S(2)}, u32[]{:S(2)}) collective-permute-start(bf16[64,32,128]{2,1,0:T(8,128)(2,1)} %get-tuple-element.10.own), channel_id=1, source_target_pairs={{1,0},{2,1},{3,2},{4,3},{5,4},{6,5},{7,6},{8,7},{9,8},{10,9},{11,1... | collective-permute-start | bytes 1572872 | tf_op jit(solution)/shard_map/ppermute | solution.py:288
  119.7 2.5 %collective-permute-start.17 = (f32[1,32,64]{2,1,0:T(8,128)S(1)}, f32[1,32,64]{2,1,0:T(8,128)S(1)}, u32[]{:S(2)}, u32[]{:S(2)}) collective-permute-start(f32[1,32,64]{2,1,0:T(8,128)S(1)} %add_bitcast_fusion), channel_id=1, source_target_pairs={{0,4},{4,0},{8,12},{12,8},{16,20},{20,16},{24,28},{28,24},{1,5},{5... | collective-permute-start | bytes 24584 | tf_op jit(solution)/shard_map/ppermute | solution.py:301
  126.4 2.3 %collective-permute-start.19 = (f32[4,32,64]{2,1,0:T(8,128)S(1)}, f32[4,32,64]{2,1,0:T(8,128)S(1)}, u32[]{:S(2)}, u32[]{:S(2)}) collective-permute-start(f32[4,32,64]{2,1,0:T(8,128)S(1)} %pad_maximum_fusion.3), channel_id=1, source_target_pairs={{0,16},{4,20},{8,24},{12,28},{16,0},{20,4},{24,8},{28,12},{1,17},{... | collective-permute-start | bytes 98312 | tf_op jit(solution)/shard_map/ppermute | solution.py:301
  128.7 8.3 %collective-permute-start.13 = (f32[8,32,64]{2,1,0:T(8,128)S(1)}, f32[8,32,64]{2,1,0:T(8,128)S(1)}, u32[]{:S(2)}, u32[]{:S(2)}) collective-permute-start(f32[8,32,64]{2,1,0:T(8,128)S(1)} %get-tuple-element.20.own), channel_id=1, source_target_pairs={{0,1},{1,2},{2,3},{3,4},{4,5},{5,6},{6,7},{7,8},{8,9},{9,10},{10,1... | collective-permute-start | bytes 196616 | tf_op jit(solution)/shard_map/ppermute | solution.py:288
  137.0 1.9 %collective-permute-start.14 = (f32[8,32,64]{2,1,0:T(8,128)S(1)}, f32[8,32,64]{2,1,0:T(8,128)S(1)}, u32[]{:S(2)}, u32[]{:S(2)}) collective-permute-start(f32[8,32,64]{2,1,0:T(8,128)S(1)} %get-tuple-element.20.own), channel_id=1, source_target_pairs={{1,0},{2,1},{3,2},{4,3},{5,4},{6,5},{7,6},{8,7},{9,8},{10,9},{11,1... | collective-permute-start | bytes 196616 | tf_op jit(solution)/shard_map/ppermute | solution.py:288
  138.9 6.1 %collective-permute-done.14.high = f32[8,32,64]{2,1,0:T(8,128)S(1)} collective-permute-done((f32[8,32,64]{2,1,0:T(8,128)S(1)}, f32[8,32,64]{2,1,0:T(8,128)S(1)}, u32[]{:S(2)}, u32[]{:S(2)}) %collective-permute-start.14) | collective-permute-done | bytes 65568 | tf_op jit(solution)/shard_map/ppermute | solution.py:288
  145.0 3.6 %middle.3.total = f32[8,32,64]{2,1,0:T(8,128)S(1)} custom-call(s32[48]{0:T(128)S(1)} %select_n.44.mid_ids, s32[6]{0:T(128)S(1)} %get-tuple-element.29.top_slots, f32[8,32,64]{2,1,0:T(8,128)S(1)} %get-tuple-element.20.own, f32[8,32,64]{2,1,0:T(8,128)S(1)} %collective-permute-done.13.low, f32[8,32,64]{2,1,0:T(8,128)S(1)} %collective-permute-done.14.high, ...), custom_call_target="tpu_custom_call" | custom-call | flops 75497472 | bytes 4718592 | tf_op jit(solution)/shard_map/middle/pallas_call | solution.py:421
  148.6 6.1 %product.3 = bf16[64,32,128]{2,1,0:T(8,128)(2,1)} custom-call(s32[512]{0:T(512)S(1)} %get-tuple-element.27.slots, f32[1]{0:T(128)S(6)} %copy.22.noise, bf16[64,32,128]{2,1,0:T(8,128)(2,1)S(1)} %collective-permute-done.11.low, bf16[64,32,128]{2,1,0:T(8,128)(2,1)S(1)} %copy-done.6, bf16[64,32,128]{2,1,0:T(8,128)(2,1)S(1)} %collective-permute-done.12.high, ...), custom_call_target="tpu_custom_call" | custom-call | flops 536870912 | bytes 33554432 | tf_op jit(solution)/shard_map/product/pallas_call | solution.py:436
  (85 shorter events, 25.1 us)
Async XLA Ops:
  0.6 104.2 %collective-permute-start = (bf16[64,32,128]{2,1,0:T(8,128)(2,1)}, bf16[64,32,128]{2,1,0:T(8,128)(2,1)S(1)}, u32[]{:S(2)}, u32[]{:S(2)}) collective-permute-start(bf16[64,32,128]{2,1,0:T(8,128)(2,1)} %own.1), channel_id=1, source_target_pairs={{0,1},{1,2},{2,3},{3,4},{4,5},{5,6},{6,7},{7,8},{8,9},{9,10},{10,1... | collective-permute-start | bytes 1572872 | tf_op jit(solution)/shard_map/ppermute | solution.py:288
  4.3 100.5 %collective-permute-start.1 = (bf16[64,32,128]{2,1,0:T(8,128)(2,1)}, bf16[64,32,128]{2,1,0:T(8,128)(2,1)}, u32[]{:S(2)}, u32[]{:S(2)}) collective-permute-start(bf16[64,32,128]{2,1,0:T(8,128)(2,1)} %own.1), channel_id=1, source_target_pairs={{1,0},{2,1},{3,2},{4,3},{5,4},{6,5},{7,6},{8,7},{9,8},{10,9},{11,1... | collective-permute-start | bytes 1572872 | tf_op jit(solution)/shard_map/ppermute | solution.py:288
  6.3 82.8 %collective-permute-start.2 = (f32[64,8,128]{2,1,0:T(8,128)}, f32[64,8,128]{2,1,0:T(8,128)S(1)}, u32[]{:S(2)}, u32[]{:S(2)}) collective-permute-start(f32[64,8,128]{2,1,0:T(8,128)} %points.1), channel_id=1, source_target_pairs={{0,1},{1,2},{2,3},{3,4},{4,5},{5,6},{6,7},{7,8},{8,9},{9,10},{10,1... | collective-permute-start | bytes 786440 | tf_op jit(solution)/shard_map/ppermute | solution.py:288
  11.7 77.4 %collective-permute-start.3 = (f32[64,8,128]{2,1,0:T(8,128)}, f32[64,8,128]{2,1,0:T(8,128)}, u32[]{:S(2)}, u32[]{:S(2)}) collective-permute-start(f32[64,8,128]{2,1,0:T(8,128)} %points.1), channel_id=1, source_target_pairs={{1,0},{2,1},{3,2},{4,3},{5,4},{6,5},{7,6},{8,7},{9,8},{10,9},{11,1... | collective-permute-start | bytes 786440 | tf_op jit(solution)/shard_map/ppermute | solution.py:288
  19.2 61.6 %copy-start.8 = (f32[8,8,64]{2,1,0:T(8,128)S(1)}, f32[8,8,64]{2,1,0:T(8,128)}, u32[]{:S(2)}) copy-start(f32[8,8,64]{2,1,0:T(8,128)} %tops.1) | copy-start | bytes 49156
  26.6 58.9 %copy-start.1 = (f32[8,64,64]{2,1,0:T(8,128)S(1)}, f32[8,64,64]{2,1,0:T(8,128)}, u32[]{:S(2)}) copy-start(f32[8,64,64]{2,1,0:T(8,128)} %top_transfer.9) | copy-start | bytes 393220
  26.6 1.8 %collective-permute-start.6 = (f32[32,64]{1,0:T(8,128)S(1)}, f32[32,64]{1,0:T(8,128)S(1)}, u32[]{:S(2)}, u32[]{:S(2)}) collective-permute-start(f32[32,64]{1,0:T(8,128)S(1)} %get-tuple-element.16), channel_id=1, source_target_pairs={{0,1},{1,0},{2,3},{3,2},{4,5},{5,4},{6,7},{7,6},{8,9},{9,8},{10,11... | collective-permute-start | bytes 24584 | tf_op jit(solution)/shard_map/ppermute | solution.py:295
  28.4 2.7 %collective-permute-start.7 = (f32[32,64]{1,0:T(8,128)S(1)}, f32[32,64]{1,0:T(8,128)S(1)}, u32[]{:S(2)}, u32[]{:S(2)}) collective-permute-start(f32[32,64]{1,0:T(8,128)S(1)} %add.43), channel_id=1, source_target_pairs={{0,2},{1,3},{2,0},{3,1},{4,6},{5,7},{6,4},{7,5},{8,10},{9,11},{10,... | collective-permute-start | bytes 24584 | tf_op jit(solution)/shard_map/ppermute | solution.py:295
  31.1 2.6 %collective-permute-start.8 = (f32[1,32,64]{2,1,0:T(8,128)S(1)}, f32[1,32,64]{2,1,0:T(8,128)S(1)}, u32[]{:S(2)}, u32[]{:S(2)}) collective-permute-start(f32[1,32,64]{2,1,0:T(8,128)S(1)} %add_bitcast_fusion.1), channel_id=1, source_target_pairs={{0,4},{4,0},{8,12},{12,8},{16,20},{20,16},{24,28},{28,24},{1,5},{5... | collective-permute-start | bytes 24584 | tf_op jit(solution)/shard_map/ppermute | solution.py:301
  33.6 19.0 %copy-start.10 = (f32[1,32,64]{2,1,0:T(8,128)}, f32[1,32,64]{2,1,0:T(8,128)S(1)}, u32[]{:S(2)}) copy-start(f32[1,32,64]{2,1,0:T(8,128)S(1)} %collective-permute-done.8) | copy-start | bytes 24580
  33.7 2.8 %collective-permute-start.9 = (f32[2,32,64]{2,1,0:T(8,128)S(1)}, f32[2,32,64]{2,1,0:T(8,128)S(1)}, u32[]{:S(2)}, u32[]{:S(2)}) collective-permute-start(f32[2,32,64]{2,1,0:T(8,128)S(1)} %pad_maximum_fusion.4), channel_id=1, source_target_pairs={{0,8},{4,12},{8,0},{12,4},{16,24},{20,28},{24,16},{28,20},{1,9},{5... | collective-permute-start | bytes 49160 | tf_op jit(solution)/shard_map/ppermute | solution.py:301
  36.5 4.1 %collective-permute-start.10 = (f32[4,32,64]{2,1,0:T(8,128)S(1)}, f32[4,32,64]{2,1,0:T(8,128)S(1)}, u32[]{:S(2)}, u32[]{:S(2)}) collective-permute-start(f32[4,32,64]{2,1,0:T(8,128)S(1)} %pad_maximum_fusion.2), channel_id=1, source_target_pairs={{0,16},{4,20},{8,24},{12,28},{16,0},{20,4},{24,8},{28,12},{1,17},{... | collective-permute-start | bytes 98312 | tf_op jit(solution)/shard_map/ppermute | solution.py:301
  40.6 31.8 %collective-permute-start.4 = (f32[8,40,64]{2,1,0:T(8,128)S(1)}, f32[8,40,64]{2,1,0:T(8,128)S(1)}, u32[]{:S(2)}, u32[]{:S(2)}) collective-permute-start(f32[8,40,64]{2,1,0:T(8,128)S(1)} %get-tuple-element.15.own), channel_id=1, source_target_pairs={{0,1},{1,2},{2,3},{3,4},{4,5},{5,6},{6,7},{7,8},{8,9},{9,10},{10,1... | collective-permute-start | bytes 245768 | tf_op jit(solution)/shard_map/ppermute | solution.py:288
  72.4 8.4 %collective-permute-start.5 = (f32[8,40,64]{2,1,0:T(8,128)S(1)}, f32[8,40,64]{2,1,0:T(8,128)S(1)}, u32[]{:S(2)}, u32[]{:S(2)}) collective-permute-start(f32[8,40,64]{2,1,0:T(8,128)S(1)} %get-tuple-element.15.own), channel_id=1, source_target_pairs={{1,0},{2,1},{3,2},{4,3},{5,4},{6,5},{7,6},{8,7},{9,8},{10,9},{11,1... | collective-permute-start | bytes 245768 | tf_op jit(solution)/shard_map/ppermute | solution.py:288
  114.1 34.5 %copy-start.6 = (bf16[64,32,128]{2,1,0:T(8,128)(2,1)S(1)}, bf16[64,32,128]{2,1,0:T(8,128)(2,1)}, u32[]{:S(2)}) copy-start(bf16[64,32,128]{2,1,0:T(8,128)(2,1)} %get-tuple-element.10.own) | copy-start | bytes 1572868
  114.1 1.2 collective-permute-start.15
  115.3 4.3 %collective-permute-start.16 = (f32[32,64]{1,0:T(8,128)S(1)}, f32[32,64]{1,0:T(8,128)S(1)}, u32[]{:S(2)}, u32[]{:S(2)}) collective-permute-start(f32[32,64]{1,0:T(8,128)S(1)} %add.45), channel_id=1, source_target_pairs={{0,2},{1,3},{2,0},{3,1},{4,6},{5,7},{6,4},{7,5},{8,10},{9,11},{10,... | collective-permute-start | bytes 24584 | tf_op jit(solution)/shard_map/ppermute | solution.py:295
  115.3 33.3 %collective-permute-start.11 = (bf16[64,32,128]{2,1,0:T(8,128)(2,1)}, bf16[64,32,128]{2,1,0:T(8,128)(2,1)S(1)}, u32[]{:S(2)}, u32[]{:S(2)}) collective-permute-start(bf16[64,32,128]{2,1,0:T(8,128)(2,1)} %get-tuple-element.10.own), channel_id=1, source_target_pairs={{0,1},{1,2},{2,3},{3,4},{4,5},{5,6},{6,7},{7,8},{8,9},{9,10},{10,1... | collective-permute-start | bytes 1572872 | tf_op jit(solution)/shard_map/ppermute | solution.py:288
  117.5 31.1 %collective-permute-start.12 = (bf16[64,32,128]{2,1,0:T(8,128)(2,1)}, bf16[64,32,128]{2,1,0:T(8,128)(2,1)S(1)}, u32[]{:S(2)}, u32[]{:S(2)}) collective-permute-start(bf16[64,32,128]{2,1,0:T(8,128)(2,1)} %get-tuple-element.10.own), channel_id=1, source_target_pairs={{1,0},{2,1},{3,2},{4,3},{5,4},{6,5},{7,6},{8,7},{9,8},{10,9},{11,1... | collective-permute-start | bytes 1572872 | tf_op jit(solution)/shard_map/ppermute | solution.py:288
  119.7 4.0 %collective-permute-start.17 = (f32[1,32,64]{2,1,0:T(8,128)S(1)}, f32[1,32,64]{2,1,0:T(8,128)S(1)}, u32[]{:S(2)}, u32[]{:S(2)}) collective-permute-start(f32[1,32,64]{2,1,0:T(8,128)S(1)} %add_bitcast_fusion), channel_id=1, source_target_pairs={{0,4},{4,0},{8,12},{12,8},{16,20},{20,16},{24,28},{28,24},{1,5},{5... | collective-permute-start | bytes 24584 | tf_op jit(solution)/shard_map/ppermute | solution.py:301
  123.6 2.8 %collective-permute-start.18 = (f32[2,32,64]{2,1,0:T(8,128)S(1)}, f32[2,32,64]{2,1,0:T(8,128)S(1)}, u32[]{:S(2)}, u32[]{:S(2)}) collective-permute-start(f32[2,32,64]{2,1,0:T(8,128)S(1)} %pad_maximum_fusion.5), channel_id=1, source_target_pairs={{0,8},{4,12},{8,0},{12,4},{16,24},{20,28},{24,16},{28,20},{1,9},{5... | collective-permute-start | bytes 49160 | tf_op jit(solution)/shard_map/ppermute | solution.py:301
  126.4 12.5 %collective-permute-start.19 = (f32[4,32,64]{2,1,0:T(8,128)S(1)}, f32[4,32,64]{2,1,0:T(8,128)S(1)}, u32[]{:S(2)}, u32[]{:S(2)}) collective-permute-start(f32[4,32,64]{2,1,0:T(8,128)S(1)} %pad_maximum_fusion.3), channel_id=1, source_target_pairs={{0,16},{4,20},{8,24},{12,28},{16,0},{20,4},{24,8},{28,12},{1,17},{... | collective-permute-start | bytes 98312 | tf_op jit(solution)/shard_map/ppermute | solution.py:301
  128.7 10.2 %collective-permute-start.13 = (f32[8,32,64]{2,1,0:T(8,128)S(1)}, f32[8,32,64]{2,1,0:T(8,128)S(1)}, u32[]{:S(2)}, u32[]{:S(2)}) collective-permute-start(f32[8,32,64]{2,1,0:T(8,128)S(1)} %get-tuple-element.20.own), channel_id=1, source_target_pairs={{0,1},{1,2},{2,3},{3,4},{4,5},{5,6},{6,7},{7,8},{8,9},{9,10},{10,1... | collective-permute-start | bytes 196616 | tf_op jit(solution)/shard_map/ppermute | solution.py:288
  137.0 8.1 %collective-permute-start.14 = (f32[8,32,64]{2,1,0:T(8,128)S(1)}, f32[8,32,64]{2,1,0:T(8,128)S(1)}, u32[]{:S(2)}, u32[]{:S(2)}) collective-permute-start(f32[8,32,64]{2,1,0:T(8,128)S(1)} %get-tuple-element.20.own), channel_id=1, source_target_pairs={{1,0},{2,1},{3,2},{4,3},{5,4},{6,5},{7,6},{8,7},{9,8},{10,9},{11,1... | collective-permute-start | bytes 196616 | tf_op jit(solution)/shard_map/ppermute | solution.py:288
  (13 other events, 87.4 us)

commit v2 on v0

v2 whole, which is shorter than its diff:
```python
import functools
import math

import jax
import jax.numpy as jnp
from jax import lax
from jax.experimental import pallas as pl
from jax.experimental.pallas import tpu as pltpu
from jax.sharding import PartitionSpec as P


MATVECS = 2
AXES = ("leaf", "sub")
F32 = jnp.float32
BF16 = jnp.bfloat16
LN2 = math.log(2.0)
DISTANCE_SCALE = math.sqrt(3.0) / LN2
MIB = 1 << 20
GROUP = 16
PARTS = 4

VMEM = pl.BlockSpec(memory_space=pltpu.VMEM)
SMEM = pl.BlockSpec(memory_space=pltpu.SMEM)
HBM = pl.BlockSpec(memory_space=pltpu.HBM)


def split(value):
    high = value.astype(BF16).astype(F32)
    rest = value - high
    mid = rest.astype(BF16).astype(F32)
    low = (rest - mid).astype(BF16).astype(F32)
    return high, mid, low


def features(terms):
    high, mid, low = terms
    pad = jnp.zeros_like(high)
    low = pad if low is None else low
    scaled = high + mid + low
    norm = jnp.sum(scaled * scaled, axis=0, keepdims=True)
    norm_high, norm_mid, norm_low = split(norm)
    row = lax.broadcasted_iota(jnp.int32, high.shape, 0)
    one = jnp.ones_like(norm)

    def rows(values):
        block = pad
        for index, value in enumerate(values):
            block = jnp.where(row == index, value, block)
        return block

    norms = (norm_high, norm_mid, norm_low)
    ones = (one, one, one)
    left = jnp.concatenate([high, high, mid, mid, high, low, rows(norms + ones), pad], axis=0)
    right = jnp.concatenate(
        [-2.0 * x for x in (high, mid, high, mid, low, high)] + [rows(ones + norms), pad], axis=0
    )
    return left, right


def kernel_of(squared, amp):
    squared = jnp.maximum(squared, 1e-20)
    root = squared * lax.rsqrt(squared)
    return (amp + (amp * LN2) * root) * jnp.exp2(-root)


def dot(a, b):
    return jnp.dot(a, b, preferred_element_type=F32)


def dot_nt(a, b):
    return lax.dot_general(a, b, (((1,), (1,)), ((), ())), preferred_element_type=F32)


def call(body, outs, in_specs, scratch=(), limit=24 * MIB, micros=1, aliases=None, out_specs=None):
    return pl.pallas_call(
        body,
        out_shape=outs,
        in_specs=in_specs,
        out_specs=out_specs if out_specs is not None else [VMEM] * len(outs),
        scratch_shapes=list(scratch),
        input_output_aliases=aliases or {},
        compiler_params=pltpu.CompilerParams(vmem_limit_bytes=limit),
        cost_estimate=pl.CostEstimate(
            flops=int(micros * 1.1e9), bytes_accessed=int(micros * 1e6), transcendentals=0
        ),
    )


def decode(items, item, near):
    code = items[item]
    slot = code & 0xFFFF
    return slot, lax.shift_right_logical(slot, near.bit_length() - 1), lax.shift_right_logical(code, 16)


def near_items(items, left, right, blocks, amp, start, count, near, part=0, parts=1):
    turns = lax.div(count + GROUP - 1, GROUP)

    def step(turn, carry):
        for inner in range(GROUP):
            item = start + jnp.minimum(turn * GROUP + inner, count - 1)
            slot, row, column = decode(items, item, near)
            blocks[slot] = kernel_of(dot(left[column], right[row]), amp).astype(BF16)
        return carry

    lax.fori_loop(lax.div(turns * part, parts), lax.div(turns * (part + 1), parts), step, 0)


def scale_block(inv_scale, shape):
    row = lax.broadcasted_iota(jnp.int32, shape, 0)
    block = jnp.zeros(shape, F32)
    for feature in range(shape[0]):
        block = jnp.where(row == feature, inv_scale[feature] * DISTANCE_SCALE, block)
    return block


def local_body(near, part, parts, items, amp, inv_scale, *refs):
    slots = items.shape[0] - 2
    if part == 0:
        points, blocks, right, left = refs
        leaves, feat, size = points.shape
        scale = scale_block(inv_scale, (feat, size))

        def step(turn, carry):
            for inner in range(8):
                leaf = turn * 8 + inner
                left_block, right_block = features(split(points[leaf] * scale))
                left[leaf] = left_block.T.astype(BF16)
                right[leaf] = right_block.astype(BF16)
            return carry

        lax.fori_loop(0, leaves // 8, step, 0)
    else:
        right, left, _, blocks = refs
    near_items(
        items, left, right, blocks, amp[0], 0, items[slots], near, part, parts
    )


def halo_body(near, items, amp, low, high, right, blocks_in, blocks, left):
    leaves, _, _ = right.shape
    feat = right.shape[1] // 8
    slots = items.shape[0] - 2

    def step(turn, carry):
        for inner in range(4):
            leaf = turn * 4 + inner
            for base, source in ((0, low), (leaves, high)):
                terms = source[leaf, : 2 * feat].astype(F32)
                left_block, _ = features((terms[:feat], terms[feat:], None))
                left[base + leaf] = left_block.T.astype(BF16)
        return carry

    lax.fori_loop(0, leaves // 4, step, 0)
    near_items(
        items, left, right, blocks, amp[0], items[slots], items[slots + 1], near
    )
    empty = jnp.zeros(blocks.shape[1:], BF16)

    def clear(item, carry):
        blocks[decode(items, item, near)[0]] = empty
        return carry

    lax.fori_loop(items[slots] + items[slots + 1], slots, clear, 0)


def pair(value, axis):
    upper = value.astype(BF16)
    lower = (value - upper.astype(F32)).astype(BF16)
    return jnp.concatenate([upper, lower], axis=axis)


def quarters(product):
    rows, columns = product.shape[0] // 2, product.shape[1] // 2
    product = product[:rows] + product[rows:]
    return product[:, :columns] + product[:, columns:]


def up_group(vector, operator, group, members):
    total = None
    for member in range(members):
        leaf = group * members + member
        term = dot_nt(vector(leaf), operator[leaf])
        total = term if total is None else total + term
    rank = total.shape[1] // 2
    return total[:, :rank] + total[:, rank:]


def up_top(coef, matrix):
    both = pair(coef, 0)
    product = dot(jnp.concatenate([both, both], axis=1), matrix)
    rows = coef.shape[0]
    return product[:rows] + product[rows:]


def prepare_body(
    members, inv_scale, points_at, probes_at, basis_at, transfer_at, top_transfer_at, skeleton_at,
    operator, packed, top, top_split,
    points, basis, transfer, top_transfer, skeleton, sems, more_sems,
):
    leaves, feat, size = points.shape
    rank = basis.shape[1]
    groups = top_split.shape[0]
    skip = 2 * feat
    scale = scale_block(inv_scale, (feat, size))

    def copies(group):
        where = pl.ds(group * members, members)
        pairs = (
            (probes_at.at[where], packed.at[where, skip:, :]),
            (basis_at.at[where], basis.at[where]),
            (transfer_at.at[where], transfer.at[where]),
        )
        return [
            pltpu.make_async_copy(source, target, sems.at[index, group])
            for index, (source, target) in enumerate(pairs)
        ]

    pairs = ((points_at, points), (skeleton_at, skeleton), (top_transfer_at, top_transfer))
    whole = [
        pltpu.make_async_copy(source, target, more_sems.at[index])
        for index, (source, target) in enumerate(pairs)
    ]
    for copy in whole:
        copy.start()
    for group in range(groups):
        for copy in copies(group):
            copy.start()
    for copy in whole:
        copy.wait()

    def step(group, total):
        for copy in copies(group):
            copy.wait()
        for member in range(members):
            leaf = group * members + member
            both = pair(transfer[leaf], 1).T
            product = dot(both, basis[leaf])
            operator[leaf] = pair(product[:rank] + product[rank:], 0)
            high, mid, _ = split(points[leaf] * scale)
            packed[leaf, :skip] = jnp.concatenate([high, mid], axis=0).astype(BF16)
        coef = up_group(lambda leaf: packed[leaf, skip:], operator, group, members)
        packed[leaves + group, skip:] = pair(coef, 1)
        high, mid, low = split(skeleton[group] * scale[:, :rank])
        packed[leaves + group, :skip, :rank] = jnp.concatenate([high, mid], axis=0).astype(BF16)
        packed[leaves + group, :skip, rank:] = jnp.concatenate([low, low], axis=0).astype(BF16)
        matrix = pair(top_transfer[group], 0)
        top_split[group] = matrix
        return total + up_top(coef, matrix)

    top[...] = lax.fori_loop(0, groups, step, jnp.zeros(top.shape, F32))


def skeleton_body(
    entries, mid_list, top_list, amp, inv_scale, own, low, high, tops, mid_out, top_out, left, right
):
    groups = right.shape[0]
    leaves = own.shape[0] - groups
    feat, rank = tops.shape[1:]
    scale = scale_block(inv_scale, (feat, rank))
    first = (lax.axis_index("leaf") * lax.axis_size("sub") + lax.axis_index("sub") - 1) * groups

    def step(turn, carry):
        for inner in range(2):
            group = turn * 2 + inner
            for place, source in enumerate((low, own, high)):
                terms = source[leaves + group, : 2 * feat].astype(F32)
                a, b = features((terms[:feat, :rank], terms[feat:, :rank], terms[:feat, rank:]))
                left[place * groups + group] = a.T.astype(BF16)
                if place == 1:
                    right[group] = b.astype(BF16)
        return carry

    lax.fori_loop(0, groups // 2, step, 0)

    def mid_step(group, carry):
        for entry in range(entries):
            index = mid_list[group, entry]
            place = jnp.where(index >= 0, index - first, groups)
            value = kernel_of(dot(left[place], right[group]), amp[0])
            value = value * jnp.where(index >= 0, 1.0, 0.0)
            mid_out[group * entries + entry] = pair(value, 1)
        return carry

    lax.fori_loop(0, groups, mid_step, 0)
    _, mine = features(split(tops[lax.axis_index("leaf")] * scale))
    mine = mine.astype(BF16)
    for entry in range(top_out.shape[0]):
        index = top_list[0, entry]
        other, _ = features(split(tops[jnp.maximum(index, 0)] * scale))
        value = kernel_of(dot(other.T.astype(BF16), mine), amp[0])
        top_out[entry] = pair(value * jnp.where(index >= 0, 1.0, 0.0), 1)


def middle_body(
    entries, summed, mid_list, top_list, own, low, high, tops, mid_coupling, top_coupling, top_split,
    total, table,
):
    groups, probe_count = total.shape[0], total.shape[1]
    rank = total.shape[2]
    shares = lax.axis_size("sub")
    first = (lax.axis_index("leaf") * shares + lax.axis_index("sub") - 1) * groups

    skip = own.shape[1] - probe_count

    def fill(group, carry):
        for place, source in enumerate((low, own, high)):
            both = source[source.shape[0] - groups + group, skip:]
            table[place * groups + group, :probe_count] = both[:, :rank]
            table[place * groups + group, probe_count:] = both[:, rank:]
        return carry

    lax.fori_loop(0, groups, fill, 0, unroll=2)
    product = None
    for entry in range(top_coupling.shape[0]):
        index = top_list[0, entry]
        if summed:
            coef = tops[jnp.where(index >= 0, index ^ lax.axis_index("leaf"), 0)]
        else:
            where = jnp.maximum(index, 0) * shares
            coef = tops[where].astype(F32)
            for share in range(1, shares):
                coef = coef + tops[where + share].astype(F32)
            coef = coef[:, :rank] + coef[:, rank:]
        term = dot(pair(coef, 0), top_coupling[entry])
        product = term if product is None else product + term
    top_local = pair(quarters(product), 0)

    def step(turn, carry):
        for inner in range(2):
            group = turn * 2 + inner
            product = dot_nt(top_local, top_split[group])
            for entry in range(entries):
                index = mid_list[group, entry]
                where = jnp.where(index >= 0, index - first, groups)
                product = product + dot(table[where], mid_coupling[group * entries + entry])
            total[group] = quarters(product)
        return carry

    lax.fori_loop(0, groups // 2, step, 0)


def product_body(
    members, near, again, near_list, noise, low, own, high, blocks, operator, total, top_split, *rest
):
    if again:
        out, wide, top, table = rest
    else:
        out, table = rest
    leaves, probe_count, points = out.shape
    rank = total.shape[2]
    groups = total.shape[0]
    skip = low.shape[1] - probe_count
    first = (lax.axis_index("leaf") * lax.axis_size("sub") + lax.axis_index("sub") - 1) * leaves

    def fill(leaf, carry):
        table[leaf] = low[leaf, skip:]
        table[leaves + leaf] = own[leaf]
        table[2 * leaves + leaf] = high[leaf, skip:]
        return carry

    lax.fori_loop(0, leaves, fill, 0, unroll=8)

    def column(leaf, entry):
        index = near_list[leaf, entry]
        return jnp.where(index >= 0, index - first, leaves)

    def step(group, carry):
        local = pair(total[group], 1)
        upper, lower = local[:, :rank], local[:, rank:]
        far = jnp.concatenate([upper, upper, lower, jnp.zeros_like(lower)], axis=1)
        for member in range(members):
            leaf = group * members + member
            gathered = [table[column(leaf, entry)] for entry in range(near)] + [far]
            near_weights = blocks[pl.ds(leaf * near, near)].reshape(near * points, points)
            weights = jnp.concatenate([near_weights, operator[leaf], operator[leaf]], axis=0)
            value = dot(jnp.concatenate(gathered, axis=1), weights)
            value = value + noise[0] * own[leaf].astype(F32)
            out[leaf] = value.astype(BF16)
            if again:
                wide[leaf] = value.astype(BF16)
        if again:
            coef = up_group(lambda leaf: out[leaf], operator, group, members)
            wide[leaves + group] = pair(coef, 1)
            carry = carry + up_top(coef, top_split[group])
        return carry

    result = lax.fori_loop(0, groups, step, jnp.zeros((probe_count, rank), F32))
    if again:
        top[...] = jnp.broadcast_to(pair(result, 1), top.shape)


def neighbours(block):
    count = lax.axis_size(AXES)
    forward = [(i, i + 1) for i in range(count - 1)]
    backward = [(target, source) for source, target in forward]
    return lax.ppermute(block, AXES, forward), lax.ppermute(block, AXES, backward)


def top_steps(partial):
    def exchange(value, axis, step):
        size = lax.axis_size(axis)
        other = lax.ppermute(value, axis, [(i, i ^ step) for i in range(size)])
        return other

    partial = partial + exchange(partial, "sub", 1)
    blocks = partial[None]
    step = 1
    while step < lax.axis_size("leaf"):
        blocks = jnp.concatenate([blocks, exchange(blocks, "leaf", step)], axis=0)
        step *= 2
    step = 2
    while step < lax.axis_size("sub"):
        blocks = blocks + exchange(blocks, "sub", step)
        step *= 2
    return blocks


def work_list(near_list, position, leaves):
    flat = near_list.reshape(-1)
    count = flat.shape[0]
    column = flat - position * leaves
    own = (column >= 0) & (column < leaves)
    kind = jnp.where(flat < 0, 2, jnp.where(own, 0, 1))
    column = jnp.where(own, column, jnp.where(column < 0, column + leaves, column))
    item = jnp.arange(count, dtype=jnp.int32)
    code = item + (jnp.where(flat < 0, 0, column) << 16)
    key = kind * count + item
    place = jnp.sum((key[:, None] > key[None, :]).astype(jnp.int32), axis=1)
    index = jnp.arange(count + 2, dtype=jnp.int32)[None, :]
    entry = jnp.where(
        index < count,
        jnp.where(place[:, None] == index, code[:, None], 0),
        (kind[:, None] == index - count).astype(jnp.int32),
    )
    return jnp.sum(entry, axis=0)


def on_device(
    points,
    probes,
    leaf_basis,
    mid_transfer,
    top_transfer,
    mid_skeleton,
    top_skeleton,
    near_list,
    mid_list,
    top_list,
    inv_scale,
    amplitude,
    noise_var,
):
    leaves, feat, size = points.shape
    groups, _, rank = mid_skeleton.shape
    probe_count = probes.shape[1]
    members = leaves // groups
    near = near_list.shape[1]
    entries = mid_list.shape[1]
    sds = jax.ShapeDtypeStruct
    slots = leaves * near
    devices = lax.axis_size(AXES)

    operator, mid, top, top_split = call(
        functools.partial(prepare_body, members),
        [
            sds((leaves, 2 * rank, size), BF16),
            sds((leaves + groups, 2 * feat + probe_count, size), BF16),
            sds((probe_count, rank), F32),
            sds((groups, 2 * rank, rank), BF16),
        ],
        [SMEM] + [HBM] * 6,
        scratch=[
            pltpu.VMEM(points.shape, F32),
            pltpu.VMEM(leaf_basis.shape, BF16),
            pltpu.VMEM(mid_transfer.shape, F32),
            pltpu.VMEM(top_transfer.shape, F32),
            pltpu.VMEM(mid_skeleton.shape, F32),
            pltpu.SemaphoreType.DMA((3, groups)),
            pltpu.SemaphoreType.DMA((3,)),
        ],
        micros=5,
        limit=67043328,
    )(inv_scale, points, probes, leaf_basis, mid_transfer, top_transfer, mid_skeleton)
    position = lax.axis_index("leaf") * lax.axis_size("sub") + lax.axis_index("sub")
    items = work_list(near_list, position, leaves)

    blocks_shape = sds((slots, size, size), BF16)
    for part in range(PARTS):
        body = functools.partial(local_body, near, part, PARTS)
        if part == 0:
            blocks, right, left = call(
                body,
                [
                    blocks_shape,
                    sds((leaves, 8 * feat, size), BF16),
                    sds((leaves, size, 8 * feat), BF16),
                ],
                [SMEM] * 3 + [VMEM],
                micros=4,
            )(items, amplitude, inv_scale, points)
        else:
            blocks = call(
                body, [blocks_shape], [SMEM] * 3 + [VMEM] * 3, aliases={5: 0}, micros=3
            )(items, amplitude, inv_scale, right, left, blocks)[0]

    vector = probes
    results = []
    for turn in range(MATVECS):
        again = turn + 1 < MATVECS
        low, high = neighbours(mid)
        if turn == 0:
            tops = top_steps(top)
        else:
            tops = lax.all_to_all(top, AXES, 0, 0, tiled=True)
        if turn == 0:
            blocks = call(
                functools.partial(halo_body, near),
                [blocks_shape],
                [SMEM] * 2 + [VMEM] * 4,
                scratch=[pltpu.VMEM((2 * leaves, size, 8 * feat), BF16)],
                aliases={5: 0},
                micros=9,
            )(items, amplitude, low, high, right, blocks)[0]
            mid_coupling, top_coupling = call(
                functools.partial(skeleton_body, entries),
                [
                    sds((groups * entries, rank, 2 * rank), BF16),
                    sds((top_list.shape[1], rank, 2 * rank), BF16),
                ],
                [SMEM] * 4 + [VMEM] * 4,
                scratch=[
                    pltpu.VMEM((3 * groups, rank, 8 * feat), BF16),
                    pltpu.VMEM((groups, 8 * feat, rank), BF16),
                ],
                micros=4,
            )(mid_list, top_list, amplitude, inv_scale, mid, low, high, top_skeleton)
        middle = call(
            functools.partial(middle_body, entries, turn == 0),
            [sds((groups, probe_count, rank), F32)],
            [SMEM] * 2 + [VMEM] * 7,
            scratch=[pltpu.VMEM((3 * groups, 2 * probe_count, rank), BF16)],
            micros=2,
        )(
            mid_list, top_list, mid, low, high, tops,
            mid_coupling, top_coupling, top_split,
        )[0]
        outs = [sds(vector.shape, BF16)]
        if again:
            outs += [
                sds((leaves + groups, probe_count, 2 * rank), BF16),
                sds((devices, probe_count, 2 * rank), BF16),
            ]
        values = call(
            functools.partial(product_body, members, near, again),
            outs,
            [SMEM] * 2 + [VMEM] * 7,
            scratch=[pltpu.VMEM((3 * leaves, probe_count, size), BF16)],
            micros=8,
        )(near_list, noise_var, low, vector, high, blocks, operator, middle, top_split)
        vector = values[0]
        results.append(vector)
        if again:
            mid, top = values[1], values[2]
    return (results[0], results[1])


def solution(mesh):
    whole = P(AXES, None, None)
    in_specs = (
        whole, whole, whole, whole, whole, whole,
        P(), P(AXES, None), P(AXES, None), P("leaf", None), P(), P(), P(),
    )

    return jax.shard_map(
        on_device, mesh=mesh, in_specs=in_specs, out_specs=(whole, whole), check_vma=False
    )
```

time: 400 us -> 131 us (0.33); the launches traced: 394 us -> 131 us
  other arithmetic: 139 us -> 2.91 us
  matrix products: 89.1 us -> 0 us
  blocking collectives: 95.2 us -> 22.6 us
  Pallas kernels: 0 us -> 55.7 us
  local copies, waits for them, and re-layouts: 38.4 us -> 26.3 us
  starting transfers between devices: 29.4 us -> 19.4 us
    dot_general x2 -> x0, other arithmetic: 127 us -> none  [on_device(): jnp.einsum('iknm,ikpm->ipn', near_blocks, wide_vector[near_local], prefer...]
    dot_general x18 -> x0, matrix products: 89.1 us -> none  [the longest x2 27.7 us: on_device(): jnp.einsum('iknm,ikpm->ipn', near_blocks, wide_vector[near_local], prefer...]
    all_gather x2 -> x0, blocking collectives: 66.6 us -> none  [on_device(): all_top = lax.all_gather(group_total[None], 'leaf', axis=0, tiled=True)]
    pallas_call x0 -> x11, Pallas kernels: none -> 55.7 us  [the longest x2 16.4 us: on_device(): call(functools.partial(product_body, members, near, again), outs, [SMEM]...]
    psum x2 -> x0, blocking collectives: 28.6 us -> none  [on_device(): group_total = lax.psum(partial_top, 'sub')]
    unnamed x78 -> x45, local copies, waits for them, and re-layouts: 1.44 us -> 26 us
    all_to_all x0 -> x1, blocking collectives: none -> 22.6 us  [on_device(): tops = lax.all_to_all(top, AXES, 0, 0, tiled=True)]
    gather x9 -> x0, local copies, waits for them, and re-layouts: 18.9 us -> none  [the longest x2 9.31 us: on_device(): wide_vector[near_local]]
  transfers between devices with their start and end apart: 12 -> 9, of which waited for: 0 -> 1; matrix products, arithmetic and copies ran while one was open for 55% -> 3% of each run, Pallas kernels for 0% -> 8%
where the time goes in v2:
time: 131 us
  Pallas kernels  55.7 us (43%)
  local copies, waits for them, and re-layouts  26.3 us (20%)
  blocking collectives  22.6 us (17%)
  starting transfers between devices  19.4 us (15%)
  other arithmetic  2.91 us (2%)
  between operations  2.36 us (2%)
    unnamed x45, local copies, waits for them, and re-layouts  26 us
    all_to_all x1, blocking collectives, on_device(): tops = lax.all_to_all(top, AXES, 0, 0, tiled=True)  22.6 us
    pallas_call x2, Pallas kernels, on_device(): call(functools.partial(product_body, members, near, again), outs, [SMEM]...  16.4 us
    ppermute x5, starting transfers between devices, exchange(): other = lax.ppermute(value, axis, [(i, i ^ step) for i in range(size)])  13 us
    pallas_call x1, Pallas kernels, on_device(): call(functools.partial(prepare_body, members), [sds((leaves, 2 * rank, si...  11.7 us
    pallas_call x3, Pallas kernels, on_device(): call(body, [blocks_shape], [SMEM] * 3 + [VMEM] * 3, aliases={5: 0}, micro...  7.63 us
    pallas_call x1, Pallas kernels, on_device(): call(functools.partial(halo_body, near), [blocks_shape], [SMEM] * 2 + [VM...  7.52 us
    pallas_call x2, Pallas kernels, on_device(): call(functools.partial(middle_body, entries, turn == 0), [sds((groups, pr...  5.14 us
  transfers between devices with their start and end apart: 9, of which 1 were waited for; matrix products, arithmetic and copies ran while one was open for 3% of the time, Pallas kernels for 8%

profile of v2, /device:TPU:0, one launch (start us, length us, event | category | flops | bytes accessed | tf_op | source)
XLA Modules:
  0.0 130.5 jit_solution(10391879970499494602)
XLA Ops:
  0.6 11.7 %shard_map.140 = (bf16[64,128,128]{2,1,0:T(8,128)(2,1)}, bf16[72,48,128]{2,1,0:T(8,128)(2,1)}, f32[32,64]{1,0:T(8,128)}, bf16[8,128,64]{2,1,0:T(8,128)(2,1)}) custom-call(f32[8]{0:T(128)} %inv_scale.11, f32[64,8,128]{2,1,0:T(8,128)} %refs_0_.1, bf16[64,32,128]{2,1,0:T(8,128)(2,1)} %own.1, bf16[64,64,128]{2,1,0:T(8,128)(2,1)} %basis_at.1, ...), custom_call_target="tpu_custom_call" | custom-call | flops 5500000256 | bytes 5000000 | tf_op jit(solution)/shard_map/pallas_call | solution.py:463
  12.3 2.5 %collective-permute-start = (bf16[72,48,128]{2,1,0:T(8,128)(2,1)}, bf16[72,48,128]{2,1,0:T(8,128)(2,1)S(1)}, u32[]{:S(2)}, u32[]{:S(2)}) collective-permute-start(bf16[72,48,128]{2,1,0:T(8,128)(2,1)} %get-tuple-element.14.own), channel_id=1, source_target_pairs={{0,1},{1,2},{2,3},{3,4},{4,5},{5,6},{6,7},{7,8},{8,9},{9,10},{10,1... | collective-permute-start | bytes 2654216 | tf_op jit(solution)/shard_map/ppermute | solution.py:396
  14.8 1.3 collective-permute-start.1
  16.1 3.2 %collective-permute-start.2 = (f32[32,64]{1,0:T(8,128)}, f32[32,64]{1,0:T(8,128)S(1)}, u32[]{:S(2)}, u32[]{:S(2)}) collective-permute-start(f32[32,64]{1,0:T(8,128)} %get-tuple-element.19), channel_id=1, source_target_pairs={{0,1},{1,0},{2,3},{3,2},{4,5},{5,4},{6,7},{7,6},{8,9},{9,8},{10,11... | collective-permute-start | bytes 24584 | tf_op jit(solution)/shard_map/ppermute | solution.py:402
  23.3 2.6 %collective-permute-start.3 = (f32[1,32,64]{2,1,0:T(8,128)S(1)}, f32[1,32,64]{2,1,0:T(8,128)S(1)}, u32[]{:S(2)}, u32[]{:S(2)}) collective-permute-start(f32[1,32,64]{2,1,0:T(8,128)S(1)} %add_bitcast_fusion), channel_id=1, source_target_pairs={{0,4},{4,0},{8,12},{12,8},{16,20},{20,16},{24,28},{28,24},{1,5},{5... | collective-permute-start | bytes 24584 | tf_op jit(solution)/shard_map/ppermute | solution.py:402
  27.4 3.3 %shard_map.141 = (bf16[512,128,128]{2,1,0:T(8,128)(2,1)S(1)}, bf16[64,64,128]{2,1,0:T(8,128)(2,1)S(1)}, bf16[64,128,64]{2,1,0:T(8,128)(2,1)S(1)}) custom-call(s32[514]{0:T(1024)S(1)} %select_reduce_fusion.items, f32[1]{0:T(128)S(6)} %copy.33.amp, f32[8]{0:T(128)S(1)} %copy-done.4, f32[64,8,128]{2,1,0:T(8,128)S(1)} %copy-done.8), custom_call_target="tpu_custom_call" | custom-call | flops 4400000000 | bytes 4000000 | tf_op jit(solution)/shard_map/pallas_call | solution.py:491
  30.8 2.1 %collective-permute-start.4 = (f32[2,32,64]{2,1,0:T(8,128)S(1)}, f32[2,32,64]{2,1,0:T(8,128)S(1)}, u32[]{:S(2)}, u32[]{:S(2)}) collective-permute-start(f32[2,32,64]{2,1,0:T(8,128)S(1)} %pad_maximum_fusion.2), channel_id=1, source_target_pairs={{0,8},{4,12},{8,0},{12,4},{16,24},{20,28},{24,16},{28,20},{1,9},{5... | collective-permute-start | bytes 49160 | tf_op jit(solution)/shard_map/ppermute | solution.py:402
  32.9 2.5 %shard_map.142.refs_2_ = bf16[512,128,128]{2,1,0:T(8,128)(2,1)S(1)} custom-call(s32[514]{0:T(1024)S(1)} %select_reduce_fusion.items, f32[1]{0:T(128)S(6)} %copy.33.amp, f32[8]{0:T(128)S(1)} %copy-done.4, bf16[64,64,128]{2,1,0:T(8,128)(2,1)S(1)} %get-tuple-element.15.refs_0_.right, ...), custom_call_target="tpu_custom_call", output_to_operand_aliasing={{}: (5, {})} | custom-call | flops 3300000000 | bytes 3000000 | tf_op jit(solution)/shard_map/pallas_call | solution.py:502
  35.5 2.4 %collective-permute-start.5 = (f32[4,32,64]{2,1,0:T(8,128)S(1)}, f32[4,32,64]{2,1,0:T(8,128)S(1)}, u32[]{:S(2)}, u32[]{:S(2)}) collective-permute-start(f32[4,32,64]{2,1,0:T(8,128)S(1)} %pad_maximum_fusion.1), channel_id=1, source_target_pairs={{0,16},{4,20},{8,24},{12,28},{16,0},{20,4},{24,8},{28,12},{1,17},{... | collective-permute-start | bytes 98312 | tf_op jit(solution)/shard_map/ppermute | solution.py:402
  37.9 2.5 %shard_map.143.refs_2_ = bf16[512,128,128]{2,1,0:T(8,128)(2,1)S(1)} custom-call(s32[514]{0:T(1024)S(1)} %select_reduce_fusion.items, f32[1]{0:T(128)S(6)} %copy.33.amp, f32[8]{0:T(128)S(1)} %copy-done.4, bf16[64,64,128]{2,1,0:T(8,128)(2,1)S(1)} %get-tuple-element.15.refs_0_.right, ...), custom_call_target="tpu_custom_call", output_to_operand_aliasing={{}: (5, {})} | custom-call | flops 3300000000 | bytes 3000000 | tf_op jit(solution)/shard_map/pallas_call | solution.py:502
  41.7 2.6 %collective-permute-start.6 = (f32[8,32,64]{2,1,0:T(8,128)S(1)}, f32[8,32,64]{2,1,0:T(8,128)S(1)}, u32[]{:S(2)}, u32[]{:S(2)}) collective-permute-start(f32[8,32,64]{2,1,0:T(8,128)S(1)} %pad_maximum_fusion), channel_id=1, source_target_pairs={{0,2},{1,3},{2,0},{3,1},{4,6},{5,7},{6,4},{7,5},{8,10},{9,11},{10,... | collective-permute-start | bytes 196616 | tf_op jit(solution)/shard_map/ppermute | solution.py:402
  44.4 2.5 %shard_map.144.blocks_in = bf16[512,128,128]{2,1,0:T(8,128)(2,1)S(1)} custom-call(s32[514]{0:T(1024)S(1)} %select_reduce_fusion.items, f32[1]{0:T(128)S(6)} %copy.33.amp, f32[8]{0:T(128)S(1)} %copy-done.4, bf16[64,64,128]{2,1,0:T(8,128)(2,1)S(1)} %get-tuple-element.15.refs_0_.right, ...), custom_call_target="tpu_custom_call", output_to_operand_aliasing={{}: (5, {})} | custom-call | flops 3300000000 | bytes 3000000 | tf_op jit(solution)/shard_map/pallas_call | solution.py:502
  46.9 5.7 %copy-done = bf16[512,128,128]{2,1,0:T(8,128)(2,1)} copy-done((bf16[512,128,128]{2,1,0:T(8,128)(2,1)}, bf16[512,128,128]{2,1,0:T(8,128)(2,1)S(1)}, u32[]{:S(2)}) %copy-start) | copy-done | bytes 16777240
  53.5 5.8 %copy-done.1 = bf16[512,128,128]{2,1,0:T(8,128)(2,1)S(1)} copy-done((bf16[512,128,128]{2,1,0:T(8,128)(2,1)S(1)}, bf16[512,128,128]{2,1,0:T(8,128)(2,1)}, u32[]{:S(2)}) %copy-start.1) | copy-done | bytes 16777240
  59.3 7.5 %shard_map.145.blocks = bf16[512,128,128]{2,1,0:T(8,128)(2,1)S(1)} custom-call(s32[514]{0:T(1024)S(1)} %select_reduce_fusion.items, f32[1]{0:T(128)S(6)} %copy.33.amp, bf16[72,48,128]{2,1,0:T(8,128)(2,1)S(1)} %collective-permute-done.low, bf16[72,48,128]{2,1,0:T(8,128)(2,1)S(1)} %collective-permute-done.1.high, ...), custom_call_target="tpu_custom_call", output_to_operand_aliasing={{}: (5, {})} | custom-call | flops 9900000256 | bytes 9000000 | tf_op jit(solution)/shard_map/pallas_call | solution.py:516
  66.8 5.7 %copy-done.2 = bf16[512,128,128]{2,1,0:T(8,128)(2,1)} copy-done((bf16[512,128,128]{2,1,0:T(8,128)(2,1)}, bf16[512,128,128]{2,1,0:T(8,128)(2,1)S(1)}, u32[]{:S(2)}) %copy-start.2) | copy-done | bytes 16777240
  72.6 4.1 %shard_map.146 = (bf16[48,64,128]{2,1,0:T(8,128)(2,1)S(1)}, bf16[6,64,128]{2,1,0:T(8,128)(2,1)S(1)}) custom-call(s32[8,6]{1,0:T(8,128)S(1)} %copy-done.10, s32[1,6]{1,0:T(1,128)S(1)} %copy-done.11, f32[1]{0:T(128)S(6)} %copy.33.amp, f32[8]{0:T(128)S(1)} %copy-done.5, bf16[72,48,128]{2,1,0:T(8,128)(2,1)S(1)} %copy-done.6, ...), custom_call_target="tpu_custom_call" | custom-call | flops 4400000000 | bytes 4000000 | tf_op jit(solution)/shard_map/pallas_call | solution.py:524
  76.8 2.5 %shard_map.147.total = f32[8,32,64]{2,1,0:T(8,128)S(1)} custom-call(s32[8,6]{1,0:T(8,128)S(1)} %copy-done.10, s32[1,6]{1,0:T(1,128)S(1)} %copy-done.11, bf16[72,48,128]{2,1,0:T(8,128)(2,1)S(1)} %copy-done.6, bf16[72,48,128]{2,1,0:T(8,128)(2,1)S(1)} %collective-permute-done.low, bf16[72,48,128]{2,1,0:T(8,128)(2,1)S(1)} %collective-permute-done.1.high, ...), custom_call_target="tpu_custom_call" | custom-call | flops 2200000000 | bytes 2000000 | tf_op jit(solution)/shard_map/pallas_call | solution.py:537
  79.3 5.8 %copy-done.3 = bf16[512,128,128]{2,1,0:T(8,128)(2,1)S(1)} copy-done((bf16[512,128,128]{2,1,0:T(8,128)(2,1)S(1)}, bf16[512,128,128]{2,1,0:T(8,128)(2,1)}, u32[]{:S(2)}) %copy-start.3) | copy-done | bytes 16777240
  85.1 9.6 %shard_map.148 = (bf16[64,32,128]{2,1,0:T(8,128)(2,1)}, bf16[72,32,128]{2,1,0:T(8,128)(2,1)S(1)}, bf16[32,32,128]{2,1,0:T(8,128)(2,1)S(1)}) custom-call(s32[64,8]{1,0:T(8,128)S(1)} %copy.27.near_list, f32[1]{0:T(128)S(6)} %copy.34.noise, bf16[72,48,128]{2,1,0:T(8,128)(2,1)S(1)} %collective-permute-done.low, bf16[64,32,128]{2,1,0:T(8,128)(2,1)S(1)} %copy-done.7, ...), custom_call_target="tpu_custom_call" | custom-call | flops 8800000000 | bytes 8000000 | tf_op jit(solution)/shard_map/pallas_call | solution.py:553
  94.8 1.3 %collective-permute-start.7 = (bf16[72,32,128]{2,1,0:T(8,128)(2,1)S(1)}, bf16[72,32,128]{2,1,0:T(8,128)(2,1)S(1)}, u32[]{:S(2)}, u32[]{:S(2)}) collective-permute-start(bf16[72,32,128]{2,1,0:T(8,128)(2,1)S(1)} %get-tuple-element.24.own), channel_id=1, source_target_pairs={{0,1},{1,2},{2,3},{3,4},{4,5},{5,6},{6,7},{7,8},{8,9},{9,10},{10,1... | collective-permute-start | bytes 1769480 | tf_op jit(solution)/shard_map/ppermute | solution.py:396
  97.4 22.6 %all_to_all.5.tops = bf16[32,32,128]{2,1,0:T(8,128)(2,1)S(1)} all-to-all(bf16[32,32,128]{2,1,0:T(8,128)(2,1)S(1)} %get-tuple-element.25), channel_id=1, replica_groups=mesh['leaf'=8,'sub'=4] {'leaf','sub'}, dimensions={0} | all-to-all | bytes 524288 | tf_op jit(solution)/shard_map/all_to_all | solution.py:514
  121.2 2.6 %shard_map.149.total = f32[8,32,64]{2,1,0:T(8,128)S(1)} custom-call(s32[8,6]{1,0:T(8,128)S(1)} %copy-done.10, s32[1,6]{1,0:T(1,128)S(1)} %copy-done.11, bf16[72,32,128]{2,1,0:T(8,128)(2,1)S(1)} %get-tuple-element.24.own, bf16[72,32,128]{2,1,0:T(8,128)(2,1)S(1)} %collective-permute-done.7.low, bf16[72,32,128]{2,1,0:T(8,128)(2,1)S(1)} %collective-permute-done.8.high, ...), custom_call_target="tpu_custom_call" | custom-call | flops 2200000000 | bytes 2000000 | tf_op jit(solution)/shard_map/pallas_call | solution.py:537
  123.8 6.7 %shard_map.150 = bf16[64,32,128]{2,1,0:T(8,128)(2,1)} custom-call(s32[64,8]{1,0:T(8,128)S(1)} %copy.27.near_list, f32[1]{0:T(128)S(6)} %copy.34.noise, bf16[72,32,128]{2,1,0:T(8,128)(2,1)S(1)} %collective-permute-done.7.low, bf16[64,32,128]{2,1,0:T(8,128)(2,1)S(1)} %copy-done.12, bf16[72,32,128]{2,1,0:T(8,128)(2,1)S(1)} %collective-permute-done.8.high, ...), custom_call_target="tpu_custom_call" | custom-call | flops 8800000000 | bytes 8000000 | tf_op jit(solution)/shard_map/pallas_call | solution.py:553
  (68 shorter events, 8.8 us)
Async XLA Ops:
  12.3 41.2 %collective-permute-start = (bf16[72,48,128]{2,1,0:T(8,128)(2,1)}, bf16[72,48,128]{2,1,0:T(8,128)(2,1)S(1)}, u32[]{:S(2)}, u32[]{:S(2)}) collective-permute-start(bf16[72,48,128]{2,1,0:T(8,128)(2,1)} %get-tuple-element.14.own), channel_id=1, source_target_pairs={{0,1},{1,2},{2,3},{3,4},{4,5},{5,6},{6,7},{7,8},{8,9},{9,10},{10,1... | collective-permute-start | bytes 2654216 | tf_op jit(solution)/shard_map/ppermute | solution.py:396
  14.8 38.7 %collective-permute-start.1 = (bf16[72,48,128]{2,1,0:T(8,128)(2,1)}, bf16[72,48,128]{2,1,0:T(8,128)(2,1)S(1)}, u32[]{:S(2)}, u32[]{:S(2)}) collective-permute-start(bf16[72,48,128]{2,1,0:T(8,128)(2,1)} %get-tuple-element.14.own), channel_id=1, source_target_pairs={{1,0},{2,1},{3,2},{4,3},{5,4},{6,5},{7,6},{8,7},{9,8},{10,9},{11,1... | collective-permute-start | bytes 2654216 | tf_op jit(solution)/shard_map/ppermute | solution.py:396
  16.1 6.4 %collective-permute-start.2 = (f32[32,64]{1,0:T(8,128)}, f32[32,64]{1,0:T(8,128)S(1)}, u32[]{:S(2)}, u32[]{:S(2)}) collective-permute-start(f32[32,64]{1,0:T(8,128)} %get-tuple-element.19), channel_id=1, source_target_pairs={{0,1},{1,0},{2,3},{3,2},{4,5},{5,4},{6,7},{7,6},{8,9},{9,8},{10,11... | collective-permute-start | bytes 24584 | tf_op jit(solution)/shard_map/ppermute | solution.py:402
  23.3 7.5 %collective-permute-start.3 = (f32[1,32,64]{2,1,0:T(8,128)S(1)}, f32[1,32,64]{2,1,0:T(8,128)S(1)}, u32[]{:S(2)}, u32[]{:S(2)}) collective-permute-start(f32[1,32,64]{2,1,0:T(8,128)S(1)} %add_bitcast_fusion), channel_id=1, source_target_pairs={{0,4},{4,0},{8,12},{12,8},{16,20},{20,16},{24,28},{28,24},{1,5},{5... | collective-permute-start | bytes 24584 | tf_op jit(solution)/shard_map/ppermute | solution.py:402
  30.8 4.7 %collective-permute-start.4 = (f32[2,32,64]{2,1,0:T(8,128)S(1)}, f32[2,32,64]{2,1,0:T(8,128)S(1)}, u32[]{:S(2)}, u32[]{:S(2)}) collective-permute-start(f32[2,32,64]{2,1,0:T(8,128)S(1)} %pad_maximum_fusion.2), channel_id=1, source_target_pairs={{0,8},{4,12},{8,0},{12,4},{16,24},{20,28},{24,16},{28,20},{1,9},{5... | collective-permute-start | bytes 49160 | tf_op jit(solution)/shard_map/ppermute | solution.py:402
  35.5 6.2 %collective-permute-start.5 = (f32[4,32,64]{2,1,0:T(8,128)S(1)}, f32[4,32,64]{2,1,0:T(8,128)S(1)}, u32[]{:S(2)}, u32[]{:S(2)}) collective-permute-start(f32[4,32,64]{2,1,0:T(8,128)S(1)} %pad_maximum_fusion.1), channel_id=1, source_target_pairs={{0,16},{4,20},{8,24},{12,28},{16,0},{20,4},{24,8},{28,12},{1,17},{... | collective-permute-start | bytes 98312 | tf_op jit(solution)/shard_map/ppermute | solution.py:402
  41.7 11.0 %copy-start.17 = (s32[64,8]{0,1:T(8,128)S(1)}, s32[64,8]{0,1:T(8,128)}, u32[]{:S(2)}) copy-start(s32[64,8]{0,1:T(8,128)} %param.20) | copy-start | bytes 6148
  41.7 11.7 %collective-permute-start.6 = (f32[8,32,64]{2,1,0:T(8,128)S(1)}, f32[8,32,64]{2,1,0:T(8,128)S(1)}, u32[]{:S(2)}, u32[]{:S(2)}) collective-permute-start(f32[8,32,64]{2,1,0:T(8,128)S(1)} %pad_maximum_fusion), channel_id=1, source_target_pairs={{0,2},{1,3},{2,0},{3,1},{4,6},{5,7},{6,4},{7,5},{8,10},{9,11},{10,... | collective-permute-start | bytes 196616 | tf_op jit(solution)/shard_map/ppermute | solution.py:402
  46.9 5.8 %copy-start = (bf16[512,128,128]{2,1,0:T(8,128)(2,1)}, bf16[512,128,128]{2,1,0:T(8,128)(2,1)S(1)}, u32[]{:S(2)}) copy-start(bf16[512,128,128]{2,1,0:T(8,128)(2,1)S(1)} %shard_map.144.blocks_in) | copy-start | bytes 50331652
  53.4 19.2 %copy-start.5 = (f32[8]{0:T(128)S(1)}, f32[8]{0:T(128)}, u32[]{:S(2)}) copy-start(f32[8]{0:T(128)} %inv_scale.11) | copy-start | bytes 100
  53.5 19.1 %copy-start.9 = (f32[8,8,64]{2,1,0:T(8,128)S(1)}, f32[8,8,64]{2,1,0:T(8,128)}, u32[]{:S(2)}) copy-start(f32[8,8,64]{2,1,0:T(8,128)} %tops.1) | copy-start | bytes 49156
  53.5 19.1 %copy-start.10 = (s32[8,6]{1,0:T(8,128)S(1)}, s32[8,6]{1,0:T(8,128)}, u32[]{:S(2)}) copy-start(s32[8,6]{1,0:T(8,128)} %mid_list.5) | copy-start | bytes 580
  53.5 19.1 %copy-start.11 = (s32[1,6]{1,0:T(1,128)S(1)}, s32[1,6]{1,0:T(1,128)}, u32[]{:S(2)}) copy-start(s32[1,6]{1,0:T(1,128)} %top_list.5) | copy-start | bytes 76
  53.5 5.8 %copy-start.1 = (bf16[512,128,128]{2,1,0:T(8,128)(2,1)S(1)}, bf16[512,128,128]{2,1,0:T(8,128)(2,1)}, u32[]{:S(2)}) copy-start(bf16[512,128,128]{2,1,0:T(8,128)(2,1)} %copy-done) | copy-start | bytes 50331652
  59.3 13.3 %copy-start.6 = (bf16[72,48,128]{2,1,0:T(8,128)(2,1)S(1)}, bf16[72,48,128]{2,1,0:T(8,128)(2,1)}, u32[]{:S(2)}) copy-start(bf16[72,48,128]{2,1,0:T(8,128)(2,1)} %get-tuple-element.14.own) | copy-start | bytes 2654212
  66.8 5.8 %copy-start.2 = (bf16[512,128,128]{2,1,0:T(8,128)(2,1)}, bf16[512,128,128]{2,1,0:T(8,128)(2,1)S(1)}, u32[]{:S(2)}) copy-start(bf16[512,128,128]{2,1,0:T(8,128)(2,1)S(1)} %shard_map.145.blocks) | copy-start | bytes 50331652
  72.6 4.1 %copy-start.16 = (bf16[8,128,64]{2,1,0:T(8,128)(2,1)S(1)}, bf16[8,128,64]{2,1,0:T(8,128)(2,1)}, u32[]{:S(2)}) copy-start(bf16[8,128,64]{2,1,0:T(8,128)(2,1)} %get-tuple-element.22.top_split) | copy-start | bytes 393220
  76.8 47.0 %slice-start = ((s8[16777216]{0:T(1024)(128)(4,1)}), s8[4194304]{0:T(1024)(128)(4,1)S(1)}, s32[]{:S(2)}) async-start(s8[16777216]{0:T(1024)(128)(4,1)} %bitcast.2), calls=%async_computation.1 | async-start | bytes 8388608
  79.3 5.8 %copy-start.3 = (bf16[512,128,128]{2,1,0:T(8,128)(2,1)S(1)}, bf16[512,128,128]{2,1,0:T(8,128)(2,1)}, u32[]{:S(2)}) copy-start(bf16[512,128,128]{2,1,0:T(8,128)(2,1)} %copy-done.2) | copy-start | bytes 50331652
  85.1 38.7 %slice-start.1 = ((s8[16777216]{0:T(1024)(128)(4,1)}), s8[4194304]{0:T(1024)(128)(4,1)S(1)}, s32[]{:S(2)}) async-start(s8[16777216]{0:T(1024)(128)(4,1)} %bitcast.2), calls=%async_computation.2 | async-start | bytes 8388608
  85.1 38.7 %slice-start.2 = ((s8[16777216]{0:T(1024)(128)(4,1)}), s8[4194304]{0:T(1024)(128)(4,1)S(1)}, s32[]{:S(2)}) async-start(s8[16777216]{0:T(1024)(128)(4,1)} %bitcast.2), calls=%async_computation.3 | async-start | bytes 8388608
  85.1 38.7 %slice-start.3 = ((s8[16777216]{0:T(1024)(128)(4,1)}), s8[4194304]{0:T(1024)(128)(4,1)S(1)}, s32[]{:S(2)}) async-start(s8[16777216]{0:T(1024)(128)(4,1)} %bitcast.2), calls=%async_computation.4 | async-start | bytes 8388608
  94.8 25.2 %collective-permute-start.7 = (bf16[72,32,128]{2,1,0:T(8,128)(2,1)S(1)}, bf16[72,32,128]{2,1,0:T(8,128)(2,1)S(1)}, u32[]{:S(2)}, u32[]{:S(2)}) collective-permute-start(bf16[72,32,128]{2,1,0:T(8,128)(2,1)S(1)} %get-tuple-element.24.own), channel_id=1, source_target_pairs={{0,1},{1,2},{2,3},{3,4},{4,5},{5,6},{6,7},{7,8},{8,9},{9,10},{10,1... | collective-permute-start | bytes 1769480 | tf_op jit(solution)/shard_map/ppermute | solution.py:396
  96.1 23.9 %collective-permute-start.8 = (bf16[72,32,128]{2,1,0:T(8,128)(2,1)S(1)}, bf16[72,32,128]{2,1,0:T(8,128)(2,1)S(1)}, u32[]{:S(2)}, u32[]{:S(2)}) collective-permute-start(bf16[72,32,128]{2,1,0:T(8,128)(2,1)S(1)} %get-tuple-element.24.own), channel_id=1, source_target_pairs={{1,0},{2,1},{3,2},{4,3},{5,4},{6,5},{7,6},{8,7},{9,8},{10,9},{11,1... | collective-permute-start | bytes 1769480 | tf_op jit(solution)/shard_map/ppermute | solution.py:396
  (7 other events, 14.4 us)
